TPU v7x, 32 devices: a whole 2x2x4 slice. The times are simulated.
32 devices in a mesh: groups: 2 (over y), expert: 4 (over z), dp: 2 (over x), inner: 2 (over core).
Axes of the slice: x: 2, y: 2, z: 4, core: 2. Of those that a mesh axis runs over, the one named last changes fastest.
Arguments:
- tokens: bfloat16 [2048, 1536], P(('groups', 'expert', 'dp'), 'inner'), parts along dimension 0, may hold values from -6 to 6
- out_grad: bfloat16 [2048, 1536], P(('groups', 'expert', 'dp'), 'inner'), parts along dimension 0, may hold values from -6 to 6
- expert_ids: int32 [2048, 8], P(('groups', 'expert', 'dp')), parts along dimension 0, may hold values from 0 to 63, all different within a row; in each aligned block of 128 rows (0 to 127, 128 to 255, ...) at most 17 rows name the same one
- gate_probs: float32 [2048, 8], P(('groups', 'expert', 'dp')), parts along dimension 0, may hold values from 0.05 to 0.5
- gate_weight: bfloat16 [64, 1536, 384], P('expert', 'inner', 'dp'), may hold values from -0.15625 to 0.15625
- up_weight: bfloat16 [64, 1536, 384], P('expert', 'inner', 'dp'), may hold values from -0.15625 to 0.15625
- down_weight: bfloat16 [64, 384, 1536], P('expert', 'dp', 'inner'), may hold values from -0.3125 to 0.3125
Outputs:
- token_grad: bfloat16 [2048, 1536], P(('groups', 'expert', 'dp'), 'inner'), parts along dimension 0
- prob_grad: float32 [2048, 8], P(('groups', 'expert', 'dp')), parts along dimension 0
- gate_weight_grad: bfloat16 [128, 1536, 384], P(('groups', 'expert'), 'inner', 'dp'), parts along dimension 0
- up_weight_grad: bfloat16 [128, 1536, 384], P(('groups', 'expert'), 'inner', 'dp'), parts along dimension 0
- down_weight_grad: bfloat16 [128, 384, 1536], P(('groups', 'expert'), 'dp', 'inner'), parts along dimension 0
There are 2 independent parts, one for each index of `groups`. A program takes and returns all parts, laid end to end along the dimension named above; an argument that names none is the same for every part. Nothing has to cross between parts.
Inputs may be any that keep to these rules, and one draw needn't show every extreme that they name: `expert_ids`: within the rows of one block of 128 tokens no expert is chosen more than 17 times, and some expert is chosen exactly 17 times in some block; a token's 8 experts differ.
All inputs are finite; a program needn't handle non-finite values.
Results may differ from a plain program's by a relative error of at most 0.015.
Values may be sent and summed in bfloat16 or wider, within the bound.
A program may use at most 192 MiB of HBM per device.

v0:
```python
import jax
import jax.numpy as jnp
from jax import lax
from jax.sharding import PartitionSpec as P


def on_device(tokens, out_grad, expert_ids, gate_probs, gate_weight, up_weight, down_weight):
    tok_rows, width_half = tokens.shape
    top_count = expert_ids.shape[1]
    per_dev = gate_weight.shape[0]
    owners = lax.axis_size("expert")
    experts = per_dev * owners
    capacity = tok_rows * top_count // experts + 1
    row_count = owners * capacity
    total_slots = experts * capacity
    pair_count = tok_rows * top_count
    chosen = expert_ids.reshape(-1)
    matches = (chosen[:, None] == jnp.arange(experts, dtype=jnp.int32)[None, :]).astype(jnp.int32)
    before = jnp.cumsum(matches, axis=0) - matches
    slot_index = jnp.sum(before * matches, axis=1)
    target = chosen % per_dev * row_count + chosen // per_dev * capacity + slot_index
    source_tok = (
        jnp.zeros((total_slots,), jnp.int32)
        .at[target]
        .set(jnp.arange(pair_count, dtype=jnp.int32) // top_count)
    )
    filled = jnp.zeros((total_slots,), jnp.bfloat16).at[target].set(1)
    slot_probs = (
        jnp.zeros((total_slots,), jnp.float32)
        .at[target]
        .set(gate_probs.reshape(-1))
        .astype(jnp.bfloat16)
    )
    sent_rows = (tokens[source_tok] * filled[:, None]).reshape(
        per_dev, owners, capacity, width_half
    )
    sent_grads = (out_grad[source_tok] * filled[:, None]).reshape(
        per_dev, owners, capacity, width_half
    )
    sent_probs = slot_probs.reshape(per_dev, owners, capacity)
    arrived_rows, arrived_grads, arrived_probs = (
        lax.all_to_all(sent_rows, "expert", split_axis=1, concat_axis=1, tiled=True),
        lax.all_to_all(sent_grads, "expert", split_axis=1, concat_axis=1, tiled=True),
        lax.all_to_all(sent_probs, "expert", split_axis=1, concat_axis=1, tiled=True),
    )
    full_gate, full_up, full_down = (
        lax.all_gather(gate_weight, "dp", axis=2, tiled=True),
        lax.all_gather(up_weight, "dp", axis=2, tiled=True),
        lax.all_gather(down_weight, "dp", axis=1, tiled=True),
    )
    expert_rows = arrived_rows.reshape(per_dev, row_count, width_half)
    gate_part = jnp.einsum(
        "jrd,jdf->jrf", expert_rows, full_gate, preferred_element_type=jnp.float32
    )
    up_part = jnp.einsum("jrd,jdf->jrf", expert_rows, full_up, preferred_element_type=jnp.float32)
    gate_sum, up_sum = (
        lax.psum(gate_part.astype(jnp.bfloat16), "inner").astype(jnp.float32),
        lax.psum(up_part.astype(jnp.bfloat16), "inner").astype(jnp.float32),
    )
    sigmoid_gate = jax.nn.sigmoid(gate_sum)
    activated = gate_sum * sigmoid_gate
    hidden = (activated * up_sum).astype(jnp.bfloat16)
    expert_grads = arrived_grads.reshape(per_dev, row_count, width_half)
    prob_col = arrived_probs.reshape(per_dev, row_count, 1).astype(jnp.float32)
    slope_part = jnp.einsum(
        "jrd,jfd->jrf", expert_grads, full_down, preferred_element_type=jnp.float32
    )
    slope_sum = lax.psum(slope_part.astype(jnp.bfloat16), "inner").astype(jnp.float32)
    scores = jnp.sum(hidden.astype(jnp.float32) * slope_sum, axis=-1)
    hidden_grad = prob_col * slope_sum
    gate_back = (
        hidden_grad * up_sum * sigmoid_gate * (1.0 + gate_sum * (1.0 - sigmoid_gate))
    ).astype(jnp.bfloat16)
    up_back = (hidden_grad * activated).astype(jnp.bfloat16)
    row_grads = jnp.einsum("jrf,jdf->jrd", gate_back, full_gate, preferred_element_type=jnp.float32)
    row_grads = (
        row_grads + jnp.einsum("jrf,jdf->jrd", up_back, full_up, preferred_element_type=jnp.float32)
    ).astype(jnp.bfloat16)
    returned_rows, returned_scores = (
        lax.all_to_all(
            row_grads.reshape(per_dev, owners, capacity, width_half),
            "expert",
            split_axis=1,
            concat_axis=1,
            tiled=True,
        ),
        lax.all_to_all(
            scores.astype(jnp.bfloat16).reshape(per_dev, owners, capacity),
            "expert",
            split_axis=1,
            concat_axis=1,
            tiled=True,
        ),
    )
    pair_rows = returned_rows.reshape(total_slots, width_half)[target]
    token_grad = jnp.sum(
        pair_rows.reshape(tok_rows, top_count, width_half).astype(jnp.float32), axis=1
    ).astype(jnp.bfloat16)
    prob_grad = returned_scores.reshape(-1)[target].astype(jnp.float32).reshape(tok_rows, top_count)
    grad_gate = jnp.einsum(
        "jrd,jrf->jdf", expert_rows, gate_back, preferred_element_type=jnp.float32
    )
    grad_up = jnp.einsum("jrd,jrf->jdf", expert_rows, up_back, preferred_element_type=jnp.float32)
    down_rows = (prob_col * expert_grads).astype(jnp.bfloat16)
    grad_down = jnp.einsum("jrf,jrd->jfd", hidden, down_rows, preferred_element_type=jnp.float32)
    summed_gate, summed_up, summed_down = (
        lax.psum_scatter(
            grad_gate.astype(jnp.bfloat16), "dp", scatter_dimension=2, tiled=True
        ).astype(jnp.float32),
        lax.psum_scatter(
            grad_up.astype(jnp.bfloat16), "dp", scatter_dimension=2, tiled=True
        ).astype(jnp.float32),
        lax.psum_scatter(
            grad_down.astype(jnp.bfloat16), "dp", scatter_dimension=1, tiled=True
        ).astype(jnp.float32),
    )
    return (
        token_grad,
        prob_grad,
        summed_gate.astype(jnp.bfloat16),
        summed_up.astype(jnp.bfloat16),
        summed_down.astype(jnp.bfloat16),
    )


def solution(mesh):
    placed = (
        P(("groups", "expert", "dp"), "inner"),
        P(("groups", "expert", "dp"), "inner"),
        P(("groups", "expert", "dp"), None),
        P(("groups", "expert", "dp"), None),
        P("expert", "inner", "dp"),
        P("expert", "inner", "dp"),
        P("expert", "dp", "inner"),
    )
    return jax.shard_map(
        on_device,
        mesh=mesh,
        in_specs=placed,
        out_specs=(
            P(("groups", "expert", "dp"), "inner"),
            P(("groups", "expert", "dp"), None),
            P(("groups", "expert"), "inner", "dp"),
            P(("groups", "expert"), "inner", "dp"),
            P(("groups", "expert"), "dp", "inner"),
        ),
        check_vma=False,
    )
```

profile of v0, /device:TPU:0, one launch (start us, length us, event | category | flops | bytes accessed | tf_op | source)
XLA Modules:
  0.0 753.7 jit_solution(1835674188766818200)
XLA Ops:
  9.8 18.0 %reduce-window.6 = s32[64,8,128]{2,1,0:T(8,128)S(1)} reduce-window(s32[64,8,128]{2,1,0:T(8,128)S(1)} %fusion.24, s32[]{:T(128)} %constant.51.clone.1), window={size=1x1x128 pad=0_0x0_0x127_0}, to_apply=%region_0.0 | reduce-window | flops 8323072 | bytes 524292 | tf_op jit(solution)/shard_map/reduce-window
  32.9 4.8 gather_fusion.1
  40.2 7.6 %scatter_custom_fusion.2 = bf16[1088]{0:T(1024)(128)(2,1)S(1)} fusion(s32[1024]{0:T(1024)S(1)} %bitcast.54, bf16[1024]{0:T(1024)(128)(2,1)S(1)} %broadcast.149, bf16[]{:T(256)} %constant.63.clone.1), kind=kCustom, calls=%fused_computation.74 | custom fusion | bytes 2178 | tf_op jit(solution)/shard_map/scatter | solution.py:27
  61.9 6.3 all-to-all-start.2
  72.1 35.3 %all-to-all-done.2 = bf16[16,4,17,768]{3,0,2,1:T(8,128)(2,1)S(1)} async-done(((bf16[16,4,17,768]{3,0,2,1:T(8,128)(2,1)}), bf16[16,4,17,768]{3,0,2,1:T(8,128)(2,1)S(1)}, u32[]{:S(2)}, u32[]{:S(2)}) %all-to-all-start.2) | async-done | bytes 1671200 | tf_op jit(solution)/shard_map/all_to_all | solution.py:42
  111.1 19.1 %all-gather.6.cloned.1.call-done = bf16[16,768,384]{1,2,0:T(8,128)(2,1)} async-done(((bf16[16,768,192]{1,2,0:T(8,128)(2,1)}), bf16[16,768,384]{1,2,0:T(8,128)(2,1)}) %all-gather.6.cloned.1.call-update) | async-done | bytes 9437200 | tf_op jit(solution)/shard_map/all_gather | solution.py:48
  130.2 7.4 convolution_convert_fusion.4
  137.7 112.2 %all-gather.8.cloned.1.call-done = bf16[16,768,384]{1,2,0:T(8,128)(2,1)} async-done(((bf16[16,768,192]{1,2,0:T(8,128)(2,1)}), bf16[16,768,384]{1,2,0:T(8,128)(2,1)}) %all-gather.8.cloned.1.call-update) | async-done | bytes 9437200 | tf_op jit(solution)/shard_map/all_gather | solution.py:47
  249.8 7.5 convolution_convert_fusion.3
  257.3 112.0 %all-gather.4.cloned.1.call-done = bf16[16,384,768]{2,1,0:T(8,128)(2,1)} async-done(((bf16[16,192,768]{2,1,0:T(8,128)(2,1)}), bf16[16,384,768]{2,1,0:T(8,128)(2,1)}) %all-gather.4.cloned.1.call-update) | async-done | bytes 9437200 | tf_op jit(solution)/shard_map/all_gather | solution.py:49
  369.3 7.5 fusion.14
  382.3 10.0 %all_to_all.25 = bf16[4,2,136]{2,1,0:T(2,128)(2,1)S(1)} all-to-all(bf16[4,2,136]{2,1,0:T(2,128)(2,1)S(1)} %reshape.281), channel_id=1, replica_groups=mesh['groups'=2,'expert'=4,'dp'=2,'inner'=2] {'expert'}, dimensions={0} | all-to-all | bytes 4352 | tf_op jit(solution)/shard_map/all_to_all | solution.py:44
  392.5 7.0 all-reduce.3.cloned.1.call-done
  399.5 8.3 %convolution_convert_fusion.2 = bf16[16,768,384]{1,2,0:T(8,128)(2,1)} fusion(bf16[16,68,768]{2,0,1:T(8,128)(2,1)S(1)} %bitcast.41, bf16[16,68,384]{2,1,0:T(8,128)(2,1)} %get-tuple-element.21, bf16[16,68,384]{2,1,0:T(8,128)(2,1)} %get-tuple-element.20, bf16[16,68,384]{2,1,0:T(8,128)(2,1)} %get-tuple-element.22, f32[16,68]{1,0:T(8,128)S(1)} %reshape.215), kind=kOutput, calls=%fused_computation.9 | convolution fusion | flops 652296192 | bytes 13619456 | tf_op jit(solution)/shard_map/jrd,jrf->jdf/dot_general | solution.py:100
  408.1 8.2 %convolution_convert_fusion.1 = bf16[16,768,384]{1,2,0:T(8,128)(2,1)} fusion(bf16[16,68,768]{2,0,1:T(8,128)(2,1)S(1)} %bitcast.42, bf16[16,68,384]{2,1,0:T(8,128)(2,1)} %get-tuple-element.20, f32[16,68]{1,0:T(8,128)S(1)} %reshape.215, bf16[16,68,384]{2,1,0:T(8,128)(2,1)} %get-tuple-element.22), kind=kOutput, calls=%fused_computation.8 | convolution fusion | flops 650207232 | bytes 12783872 | tf_op jit(solution)/shard_map/jrd,jrf->jdf/dot_general | solution.py:103
  417.4 7.6 %convolution_convert_fusion = bf16[16,384,768]{2,1,0:T(8,128)(2,1)} fusion(bf16[16,68,768]{2,0,1:T(8,128)(2,1)S(1)} %multiply_convert_fusion, bf16[16,68,384]{2,1,0:T(8,128)(2,1)} %get-tuple-element.21, bf16[16,68,384]{2,1,0:T(8,128)(2,1)S(1)} %copy-done.4), kind=kOutput, calls=%fused_computation.7 | convolution fusion | flops 649789440 | bytes 12779520 | tf_op jit(solution)/shard_map/jrf,jrd->jfd/dot_general | solution.py:105
  429.1 4.8 all-to-all-start.4
  433.9 6.1 fusion.41
  444.1 5.3 all-to-all-start.3
  449.7 6.8 gather_fusion.3
  457.3 31.1 %all-to-all-done.3 = bf16[16,4,17,768]{3,0,2,1:T(8,128)(2,1)S(1)} async-done(((bf16[16,4,17,768]{3,0,2,1:T(8,128)(2,1)}), bf16[16,4,17,768]{3,0,2,1:T(8,128)(2,1)S(1)}, u32[]{:S(2)}, u32[]{:S(2)}) %all-to-all-start.3) | async-done | bytes 1671200 | tf_op jit(solution)/shard_map/all_to_all | solution.py:80
  498.9 20.7 %reduce-scatter.4.cloned.1.call-done = bf16[16,768,192]{1,2,0:T(8,128)(2,1)} async-done(((bf16[16,768,384]{1,2,0:T(8,128)(2,1)}), bf16[16,768,192]{1,2,0:T(8,128)(2,1)}) %reduce-scatter.4.cloned.1.call-update) | async-done | bytes 4718608 | tf_op jit(solution)/shard_map/reduce_scatter | solution.py:107
  519.6 113.3 %reduce-scatter.6.cloned.1.call-done = bf16[16,768,192]{1,2,0:T(8,128)(2,1)} async-done(((bf16[16,768,384]{1,2,0:T(8,128)(2,1)}), bf16[16,768,192]{1,2,0:T(8,128)(2,1)}) %reduce-scatter.6.cloned.1.call-update) | async-done | bytes 4718608 | tf_op jit(solution)/shard_map/reduce_scatter | solution.py:110
  633.0 113.5 %reduce-scatter.8.cloned.1.call-done = bf16[16,192,768]{2,1,0:T(8,128)(2,1)} async-done(((bf16[16,384,768]{2,1,0:T(8,128)(2,1)}), bf16[16,192,768]{2,1,0:T(8,128)(2,1)}) %reduce-scatter.8.cloned.1.call-update) | async-done | bytes 4718608 | tf_op jit(solution)/shard_map/reduce_scatter | solution.py:113
  (91 shorter events, 58.4 us)
Async XLA Ops:
  7.2 25.7 %copy-start = (bf16[128,768]{1,0:T(8,128)(2,1)S(1)}, bf16[128,768]{1,0:T(8,128)(2,1)}, u32[]{:S(2)}) copy-start(bf16[128,768]{1,0:T(8,128)(2,1)} %param.7) | copy-start | bytes 589828
  7.2 123.1 %all-gather.6.cloned.1.call-start = ((), (), s32[]{:S(2)}) async-start(), calls=%async_computation.9 | async-start | bytes 14155776 | tf_op jit(solution)/shard_map/all_gather | solution.py:48
  7.9 241.9 %all-gather.8.cloned.1.call-start = ((), (), s32[]{:S(2)}) async-start(), calls=%async_computation.10 | async-start | bytes 14155776 | tf_op jit(solution)/shard_map/all_gather | solution.py:47
  8.7 0.7 copy-start.5
  8.7 360.6 %all-gather.4.cloned.1.call-start = ((), (), s32[]{:S(2)}) async-start(), calls=%async_computation.8 | async-start | bytes 14155776 | tf_op jit(solution)/shard_map/all_gather | solution.py:49
  37.7 10.3 %copy-start.2 = (bf16[128,768]{1,0:T(8,128)(2,1)S(1)}, bf16[128,768]{1,0:T(8,128)(2,1)}, u32[]{:S(2)}) copy-start(bf16[128,768]{1,0:T(8,128)(2,1)} %param.8) | copy-start | bytes 589828
  61.9 45.4 %all-to-all-start.2 = ((bf16[16,4,17,768]{3,0,2,1:T(8,128)(2,1)}), bf16[16,4,17,768]{3,0,2,1:T(8,128)(2,1)S(1)}, u32[]{:S(2)}, u32[]{:S(2)}) async-start(bf16[16,4,17,768]{3,0,2,1:T(8,128)(2,1)} %copy.58), calls=%async_computation.2 | async-start | bytes 3342336 | tf_op jit(solution)/shard_map/all_to_all | solution.py:42
  107.3 150.0 %all-to-all-start.1 = ((bf16[16,4,17,768]{3,0,2,1:T(8,128)(2,1)}), bf16[16,4,17,768]{3,0,2,1:T(8,128)(2,1)S(1)}, u32[]{:S(2)}, u32[]{:S(2)}) async-start(bf16[16,4,17,768]{3,0,2,1:T(8,128)(2,1)} %copy.56), calls=%async_computation.1 | async-start | bytes 3342336 | tf_op jit(solution)/shard_map/all_to_all | solution.py:43
  110.9 288.5 %all-reduce.3.cloned.1.call-start = ((), (), s32[]{:S(2)}) async-start(), calls=%async_computation.14 | async-start | bytes 5308416 | tf_op jit(solution)/shard_map/psum | solution.py:68
  376.8 0.7 copy-start.6
  376.8 142.8 %reduce-scatter.4.cloned.1.call-start = ((), (), s32[]{:S(2)}) async-start(), calls=%async_computation.11 | async-start | bytes 14155776 | tf_op jit(solution)/shard_map/reduce_scatter | solution.py:107
  407.8 225.2 %reduce-scatter.6.cloned.1.call-start = ((), (), s32[]{:S(2)}) async-start(), calls=%async_computation.12 | async-start | bytes 14155776 | tf_op jit(solution)/shard_map/reduce_scatter | solution.py:110
  416.3 1.2 copy-start.4
  416.3 330.1 %reduce-scatter.8.cloned.1.call-start = ((), (), s32[]{:S(2)}) async-start(), calls=%async_computation.13 | async-start | bytes 14155776 | tf_op jit(solution)/shard_map/reduce_scatter | solution.py:113
  425.0 1.2 copy-start.3
  426.2 13.8 %slice-start = ((s8[9437184]{0:T(1024)(128)(4,1)}), s8[1048576]{0:T(1024)(128)(4,1)S(1)}, s32[]{:S(2)}) async-start(s8[9437184]{0:T(1024)(128)(4,1)} %bitcast.44), calls=%async_computation.15 | async-start | bytes 2097152
  429.1 15.0 %all-to-all-start.4 = ((bf16[4,2,136]{2,1,0:T(2,128)(2,1)}), bf16[4,2,136]{2,1,0:T(2,128)(2,1)S(1)}, u32[]{:S(2)}, u32[]{:S(2)}) async-start(bf16[4,2,136]{2,1,0:T(2,128)(2,1)} %reshape.283), calls=%async_computation.4 | async-start | bytes 8192 | tf_op jit(solution)/shard_map/all_to_all | solution.py:87
  433.9 6.1 slice-start.1
  433.9 6.7 slice-start.2
  444.1 44.3 %all-to-all-start.3 = ((bf16[16,4,17,768]{3,0,2,1:T(8,128)(2,1)}), bf16[16,4,17,768]{3,0,2,1:T(8,128)(2,1)S(1)}, u32[]{:S(2)}, u32[]{:S(2)}) async-start(bf16[16,4,17,768]{3,0,2,1:T(8,128)(2,1)} %bitcast.6), calls=%async_computation.3 | async-start | bytes 3342336 | tf_op jit(solution)/shard_map/all_to_all | solution.py:80
  493.2 253.3 %copy-start.1 = (bf16[128,768]{1,0:T(8,128)(2,1)S(1)}, bf16[128,768]{1,0:T(8,128)(2,1)}, u32[]{:S(2)}) copy-start(bf16[128,768]{1,0:T(8,128)(2,1)} %param.7) | copy-start | bytes 589828
Sparse Core Ops, SparseCore 0:
  9.6 120.6 all-gather.5
  131.8 117.9 all-gather.7
  251.4 117.8 all-gather.3
  376.9 22.4 all-reduce.2
  407.9 111.6 reduce-scatter.3
  522.4 110.5 reduce-scatter.5
  635.9 110.5 reduce-scatter.7
where the time goes:
time: 762 us; the launch traced here: 754 us
  waiting for transfers between devices  566 us (74%)
  local copies, waits for them, and re-layouts  61.4 us (8%)
  matrix products  54.5 us (7%)
  other arithmetic  25.9 us (3%)
  starting transfers between devices  20.7 us (3%)
  between operations  14.9 us (2%)
  blocking collectives  10 us (1%)
    reduce_scatter x1, waiting for transfers between devices, on_device(): lax.psum_scatter(grad_down.astype(jnp.bfloat16), 'dp', scatter_dimension=...  113 us
    reduce_scatter x1, waiting for transfers between devices, on_device(): lax.psum_scatter(grad_up.astype(jnp.bfloat16), 'dp', scatter_dimension=2,...  113 us
    all_gather x1, waiting for transfers between devices, on_device(): lax.all_gather(gate_weight, 'dp', axis=2, tiled=True)  112 us
    all_gather x1, waiting for transfers between devices, on_device(): lax.all_gather(down_weight, 'dp', axis=1, tiled=True)  112 us
    all_to_all x1, waiting for transfers between devices, on_device(): lax.all_to_all(sent_rows, 'expert', split_axis=1, concat_axis=1, tiled=True)  35.3 us
    all_to_all x1, waiting for transfers between devices, on_device(): lax.all_to_all(row_grads.reshape(per_dev, owners, capacity, width_half),...  31.1 us
    reduce_scatter x1, waiting for transfers between devices, on_device(): lax.psum_scatter(grad_gate.astype(jnp.bfloat16), 'dp', scatter_dimension=...  20.7 us
    all_gather x1, waiting for transfers between devices, on_device(): lax.all_gather(up_weight, 'dp', axis=2, tiled=True)  19.1 us
  transfers between devices with their start and end apart: 11, of which 9 were waited for; matrix products, arithmetic and copies ran while one was open for 16% of the time, Pallas kernels for 0%

commit v1 on v0

v1 whole, which is shorter than its diff:
```python
import jax
import jax.numpy as jnp
from jax import lax
from jax.sharding import PartitionSpec as P

F32 = jnp.float32
BF16 = jnp.bfloat16


def select_rows(packed, width, top_count, per_dev, block_rows, capacity):
    total = packed.shape[0]
    blocks = total // block_rows
    run = 4 if blocks % 4 == 0 else 1
    runs = blocks // run
    span = run * block_rows
    rows = -(-run * capacity // 16) * 16
    ids = packed[:, 2 * width : 2 * width + top_count].astype(jnp.int32)
    probs = packed[:, 2 * width + top_count : 2 * width + 2 * top_count]
    mine = lax.axis_index("expert") * per_dev + jnp.arange(per_dev, dtype=jnp.int32)
    hits = ids[:, :, None] == mine[None, None, :]
    member = jnp.any(hits, axis=1).reshape(runs, span, per_dev)
    weight = jnp.sum(jnp.where(hits, probs[:, :, None].astype(F32), 0.0), axis=1)
    weight = weight.reshape(runs, span, per_dev)
    at = jnp.arange(span, dtype=jnp.int32)
    earlier = (at[:, None] > at[None, :]).astype(BF16)
    slot = jnp.einsum("ts,gse->get", earlier, member.astype(BF16), preferred_element_type=F32)
    slot = jnp.where(member.transpose(0, 2, 1), slot.astype(jnp.int32), -1)
    places = jnp.arange(rows, dtype=jnp.int32)
    picked = slot[:, :, None, :] == places[None, None, :, None]
    row_prob = jnp.sum(jnp.where(picked, weight.transpose(0, 2, 1)[:, :, None, :], 0.0), axis=3)
    return picked.astype(BF16), row_prob, hits, runs, span, rows


def on_device(tokens, out_grad, expert_ids, gate_probs, gate_weight, up_weight, down_weight):
    tok_rows, width = tokens.shape
    top_count = expert_ids.shape[1]
    per_dev = gate_weight.shape[0]
    experts = per_dev * lax.axis_size("expert")
    capacity = tok_rows * top_count // experts + 1
    packed = jnp.concatenate(
        [tokens, out_grad, expert_ids.astype(BF16), gate_probs.astype(BF16)], axis=1
    )
    packed = lax.all_gather(packed, ("expert", "dp"), axis=0, tiled=True)
    picked, row_prob, hits, runs, span, rows = select_rows(
        packed, width, top_count, per_dev, tok_rows, capacity
    )
    both = packed[:, : 2 * width].reshape(runs, span, 2 * width)
    sorted_rows = jnp.einsum("gest,gtd->egsd", picked, both, preferred_element_type=F32)
    sorted_rows = sorted_rows.astype(BF16).reshape(per_dev, runs * rows, 2 * width)
    expert_rows, expert_grads = sorted_rows[:, :, :width], sorted_rows[:, :, width:]
    prob_col = row_prob.transpose(1, 0, 2).reshape(per_dev, runs * rows, 1)
    hid = gate_weight.shape[2]
    parts = jnp.concatenate(
        [
            jnp.einsum("jrd,jdf->jrf", expert_rows, gate_weight, preferred_element_type=F32),
            jnp.einsum("jrd,jdf->jrf", expert_rows, up_weight, preferred_element_type=F32),
            jnp.einsum("jrd,jfd->jrf", expert_grads, down_weight, preferred_element_type=F32),
        ],
        axis=2,
    ).astype(BF16)
    sums = lax.psum(parts, "inner").astype(F32)
    gate, up, slope = sums[..., :hid], sums[..., hid : 2 * hid], sums[..., 2 * hid :]
    sig = jax.nn.sigmoid(gate)
    act = gate * sig
    hidden = (act * up).astype(BF16)
    scores = jnp.sum(hidden.astype(F32) * slope, axis=-1)
    hidden_grad = prob_col * slope
    gate_back = (hidden_grad * up * sig * (1.0 + gate * (1.0 - sig))).astype(BF16)
    up_back = (hidden_grad * act).astype(BF16)
    row_grads = jnp.einsum("jrf,jdf->jrd", gate_back, gate_weight, preferred_element_type=F32)
    row_grads = (
        row_grads + jnp.einsum("jrf,jdf->jrd", up_back, up_weight, preferred_element_type=F32)
    ).astype(BF16)
    token_part = jnp.einsum(
        "gest,egsd->gtd",
        picked,
        row_grads.reshape(per_dev, runs, rows, width),
        preferred_element_type=F32,
    ).reshape(runs * span, width)
    score_rows = scores.reshape(per_dev, runs, rows).transpose(1, 0, 2)
    score_part = jnp.sum(picked.astype(F32) * score_rows[..., None], axis=2)
    score_part = score_part.transpose(0, 2, 1).reshape(runs * span, 1, per_dev)
    score_part = jnp.sum(jnp.where(hits, score_part, 0.0), axis=2)
    returned = lax.psum_scatter(
        jnp.concatenate([token_part, score_part], axis=1).astype(BF16),
        ("expert", "dp"),
        scatter_dimension=0,
        tiled=True,
    )
    grad_gate = jnp.einsum("jrd,jrf->jdf", expert_rows, gate_back, preferred_element_type=F32)
    grad_up = jnp.einsum("jrd,jrf->jdf", expert_rows, up_back, preferred_element_type=F32)
    down_rows = (prob_col * expert_grads.astype(F32)).astype(BF16)
    grad_down = jnp.einsum("jrf,jrd->jfd", hidden, down_rows, preferred_element_type=F32)
    return (
        returned[:, :width],
        returned[:, width:].astype(F32),
        grad_gate.astype(BF16),
        grad_up.astype(BF16),
        grad_down.astype(BF16),
    )


def solution(mesh):
    placed = (
        P(("groups", "expert", "dp"), "inner"),
        P(("groups", "expert", "dp"), "inner"),
        P(("groups", "expert", "dp"), None),
        P(("groups", "expert", "dp"), None),
        P("expert", "inner", "dp"),
        P("expert", "inner", "dp"),
        P("expert", "dp", "inner"),
    )
    return jax.shard_map(
        on_device,
        mesh=mesh,
        in_specs=placed,
        out_specs=(
            P(("groups", "expert", "dp"), "inner"),
            P(("groups", "expert", "dp"), None),
            P(("groups", "expert"), "inner", "dp"),
            P(("groups", "expert"), "inner", "dp"),
            P(("groups", "expert"), "dp", "inner"),
        ),
        check_vma=False,
    )
```

time: 762 us -> 244 us (0.32)
  waiting for transfers between devices: 566 us -> 140 us
  local copies, waits for them, and re-layouts: 61.4 us -> 19.9 us
  starting transfers between devices: 20.7 us -> 0.12 us
  blocking collectives: 10 us -> 0 us
    reduce_scatter x3 -> x0, waiting for transfers between devices: 248 us -> none  [the longest x1 113 us: on_device(): lax.psum_scatter(grad_down.astype(jnp.bfloat16), 'dp', scatter_dimension=...]
    all_gather x3 -> x1, waiting for transfers between devices: 243 us -> 66.2 us  [on_device(): packed = lax.all_gather(packed, ('expert', 'dp'), axis=0, tiled=True)]
    all_to_all x4 -> x0, waiting for transfers between devices: 66.4 us -> none  [the longest x1 35.3 us: on_device(): lax.all_to_all(sent_rows, 'expert', split_axis=1, concat_axis=1, tiled=True)]
    unnamed x7 -> x4, waiting for transfers between devices: 2.12 us -> 52 us
    gather x6 -> x0, local copies, waits for them, and re-layouts: 26.5 us -> none  [the longest x2 8.39 us: on_device(): out_grad[source_tok] * filled[:, None]]
    all_to_all x4 -> x0, starting transfers between devices: 20.1 us -> none  [the longest x1 6.32 us: on_device(): lax.all_to_all(sent_rows, 'expert', split_axis=1, concat_axis=1, tiled=True)]
    another operation x3 -> x0, other arithmetic: 18.2 us -> none
    scatter x3 -> x0, local copies, waits for them, and re-layouts: 16.2 us -> none  [the longest x1 7.59 us: on_device(): filled = jnp.zeros((total_slots,), jnp.bfloat16).at[target].set(1)]
  transfers between devices with their start and end apart: 11 -> 3, of which waited for: 9 -> 3; matrix products, arithmetic and copies ran while one was open for 16% -> 6% of each run, Pallas kernels for 0% -> 0%
where the time goes in v1:
time: 244 us; the launch traced here: 243 us
  waiting for transfers between devices  140 us (57%)
  matrix products  47.4 us (19%)
  other arithmetic  21.9 us (9%)
  local copies, waits for them, and re-layouts  19.9 us (8%)
  between operations  14 us (6%)
    all_gather x1, waiting for transfers between devices, on_device(): packed = lax.all_gather(packed, ('expert', 'dp'), axis=0, tiled=True)  66.2 us
    unnamed x4, waiting for transfers between devices  52 us
    psum x1, waiting for transfers between devices, on_device(): sums = lax.psum(parts, 'inner').astype(F32)  21.5 us
    dot_general x1, matrix products, on_device(): jnp.einsum('gest,gtd->egsd', picked, both, preferred_element_type=F32)  8.22 us
    dot_general x1, matrix products, on_device(): jnp.einsum('jrd,jfd->jrf', expert_grads, down_weight, preferred_element_t...  6.93 us
    unnamed x18, local copies, waits for them, and re-layouts  6.4 us
    dot_general x1, matrix products, on_device(): jnp.einsum('jrd,jrf->jdf', expert_rows, gate_back, preferred_element_type...  5.93 us
    dot_general x1, matrix products, on_device(): jnp.einsum('jrd,jrf->jdf', expert_rows, up_back, preferred_element_type=F32)  5.92 us
  transfers between devices with their start and end apart: 3, of which 3 were waited for; matrix products, arithmetic and copies ran while one was open for 6% of the time, Pallas kernels for 0%

profile of v1, /device:TPU:0, one launch (start us, length us, event | category | flops | bytes accessed | tf_op | source)
XLA Modules:
  0.0 243.1 jit_solution(7060287537651137806)
XLA Ops:
  11.6 66.2 %all-gather.2.cloned.1.call-done = bf16[1024,1552]{0,1:T(8,128)(2,1)} async-done(((bf16[128,1552]{0,1:T(8,128)(2,1)}), bf16[1024,1552]{0,1:T(8,128)(2,1)}) %all-gather.2.cloned.1.call-update) | async-done | bytes 3178512 | tf_op jit(solution)/shard_map/all_gather | solution.py:43
  79.0 1.6 slice-done.2
  80.6 2.9 %copy.79 = bf16[1024,1536]{1,0:T(8,128)(2,1)} copy(bf16[1024,1536]{0,1:T(8,128)(2,1)S(1)} %slice-done.2) | data formatting | bytes 6291456 | tf_op jit(solution)/shard_map/reshape | solution.py:47
  83.6 8.2 %convert_bitcast_fusion = bf16[16,2,80,1536]{3,2,0,1:T(8,128)(2,1)} fusion(bf16[2,512,1536,1]{2,1,3,0:T(8,128)(2,1)} %bitcast.58, s32[2,16,512]{2,1,0:T(8,128)S(1)} %fusion.29), kind=kOutput, calls=%fused_computation.2 | convolution fusion | flops 4031774720 | bytes 11075584 | tf_op jit(solution)/shard_map/gest,gtd->egsd/dot_general | solution.py:48
  91.8 3.7 %copy.71 = bf16[16,2,80,1536]{3,2,1,0:T(8,128)(2,1)S(1)} copy(bf16[16,2,80,1536]{3,2,0,1:T(8,128)(2,1)} %convert_bitcast_fusion) | data formatting | bytes 15728640 | tf_op jit(solution)/shard_map/convert_element_type | solution.py:49
  95.5 6.9 %fusion.26 = bf16[16,160,192]{2,1,0:T(8,128)(2,1)S(1)} fusion(bf16[16,192,768]{2,1,0:T(8,128)(2,1)} %param.13, bf16[16,160,1536]{2,1,0:T(8,128)(2,1)S(1)} %bitcast.47), kind=kOutput, calls=%fused_computation.36 | convolution fusion | flops 755466240 | bytes 9633792 | tf_op jit(solution)/shard_map/jrd,jfd->jrf/dot_general | solution.py:57
  102.5 4.1 %fusion.23 = bf16[16,160,192]{2,1,0:T(8,128)(2,1)S(1)} fusion(bf16[16,768,192]{1,2,0:T(8,128)(2,1)} %param.12, bf16[16,160,1536]{2,1,0:T(8,128)(2,1)S(1)} %bitcast.48), kind=kOutput, calls=%fused_computation.35 | convolution fusion | flops 755466240 | bytes 9633792 | tf_op jit(solution)/shard_map/jrd,jdf->jrf/dot_general | solution.py:56
  106.6 4.0 %fusion.20 = bf16[16,160,192]{2,1,0:T(8,128)(2,1)S(1)} fusion(bf16[16,768,192]{1,2,0:T(8,128)(2,1)} %param.11, bf16[16,160,1536]{2,1,0:T(8,128)(2,1)S(1)} %bitcast.49), kind=kOutput, calls=%fused_computation.34 | convolution fusion | flops 755466240 | bytes 9633792 | tf_op jit(solution)/shard_map/jrd,jdf->jrf/dot_general | solution.py:55
  110.6 2.8 %pad_maximum_fusion = bf16[16,160,576]{2,1,0:T(8,128)(2,1)} fusion(bf16[16,160,192]{2,1,0:T(8,128)(2,1)S(1)} %fusion.26, bf16[16,160,192]{2,1,0:T(8,128)(2,1)S(1)} %fusion.23, bf16[16,160,192]{2,1,0:T(8,128)(2,1)S(1)} %fusion.20), kind=kLoop, calls=%fused_computation.14 | loop fusion | flops 8847360 | bytes 5898240 | tf_op jit(solution)/shard_map/concatenate | solution.py:53
  113.7 21.5 %all-reduce.2.cloned.1.call-done = bf16[16,160,576]{2,1,0:T(8,128)(2,1)} async-done(((bf16[16,160,576]{2,1,0:T(8,128)(2,1)}), bf16[16,160,576]{2,1,0:T(8,128)(2,1)}) %all-reduce.2.cloned.1.call-update) | async-done | bytes 2949136 | tf_op jit(solution)/shard_map/psum | solution.py:61
  135.2 2.6 %convert_element_type.75 = f32[16,160,576]{2,1,0:T(8,128)S(1)} convert(bf16[16,160,576]{2,1,0:T(8,128)(2,1)} %all-reduce.2.cloned.1.call-done) | non-fusion elementwise | flops 1474560 | bytes 8847360 | tf_op jit(solution)/shard_map/convert_element_type | solution.py:61
  137.8 2.7 %multiply_reduce_fusion.1 = (f32[16,160]{1,0:T(8,128)S(1)}, bf16[16,160,192]{2,1,0:T(8,128)(2,1)}) fusion(f32[16,160,576]{2,1,0:T(8,128)S(1)} %convert_element_type.75), kind=kLoop, calls=%fused_computation.19 | loop fusion | flops 4421120 | bytes 6891520 | tf_op jit(solution)/shard_map/reduce_sum | solution.py:66
  141.1 2.5 %select_reduce_fusion = (f32[2,16,80]{2,1,0:T(8,128)S(1)}, f32[2,16,512]{2,1,0:T(8,128)S(1)}) fusion(f32[2,16,512]{2,1,0:T(8,128)S(1)} %copy.68, s32[2,16,512]{2,1,0:T(8,128)S(1)} %fusion.29, f32[2,16,80]{2,1,0:T(8,128)S(1)} %copy.73), kind=kLoop, calls=%fused_computation.4 | loop fusion | flops 9156096 | bytes 217088 | tf_op jit(solution)/shard_map/reduce_sum | solution.py:30
  143.8 4.7 %multiply_convert_fusion.5 = (bf16[16,160,192]{2,1,0:T(8,128)(2,1)S(1)}, bf16[16,160,192]{2,1,0:T(8,128)(2,1)S(1)}) fusion(f32[16,160,576]{2,1,0:T(8,128)} %copy-done, f32[16,160]{1,0:T(8,128)S(1)} %mul.54), kind=kLoop, calls=%fused_computation.21 | loop fusion | flops 6881280 | bytes 7874560 | tf_op jit(solution)/shard_map/convert_element_type | solution.py:69
  148.6 3.6 %fusion.36 = f32[16,160,768]{2,1,0:T(8,128)S(1)} fusion(bf16[16,160,192]{2,1,0:T(8,128)(2,1)S(1)} %get-tuple-element.40, bf16[16,768,192]{1,2,0:T(8,128)(2,1)} %param.11), kind=kOutput, calls=%fused_computation.54 | convolution fusion | flops 754974720 | bytes 13565952 | tf_op jit(solution)/shard_map/jrf,jdf->jrd/dot_general | solution.py:70
  153.4 3.7 %bitcast_convert_fusion = bf16[2,512,768]{2,1,0:T(8,128)(2,1)} fusion(bf16[16,2,80,768]{3,2,1,0:T(8,128)(2,1)S(1)} %bitcast.57, s32[2,16,512]{2,1,0:T(8,128)S(1)} %fusion.29), kind=kOutput, calls=%fused_computation.15 | convolution fusion | flops 2015363072 | bytes 5570560 | tf_op jit(solution)/shard_map/gest,egsd->gtd/dot_general | solution.py:74
  157.1 2.6 %copy.75 = bf16[1024,768]{0,1:T(8,128)(2,1)} copy(bf16[1024,768]{1,0:T(8,128)(2,1)} %bitcast.59) | data formatting | bytes 3145728 | tf_op jit(solution)/shard_map/reshape | solution.py:79
  159.7 2.7 %pad_maximum_fusion.1 = bf16[1024,776]{0,1:T(8,128)(2,1)} fusion(bf16[1024,8]{0,1:T(8,128)(2,1)S(1)} %fusion.33, bf16[1024,768]{0,1:T(8,128)(2,1)} %copy.75), kind=kLoop, calls=%fused_computation.37 | loop fusion | flops 3178496 | bytes 3178496 | tf_op jit(solution)/shard_map/concatenate | solution.py:85
  162.4 3.7 %copy.80 = bf16[1024,776]{1,0:T(8,128)(2,1)} copy(bf16[1024,776]{0,1:T(8,128)(2,1)} %pad_maximum_fusion.1) | data formatting | bytes 3178496
  166.1 5.9 %convolution_convert_fusion.1 = bf16[16,768,192]{1,2,0:T(8,128)(2,1)} fusion(bf16[16,160,192]{2,1,0:T(8,128)(2,1)S(1)} %get-tuple-element.40, bf16[16,160,1536]{2,1,0:T(8,128)(2,1)} %bitcast.50), kind=kOutput, calls=%fused_computation.18 | convolution fusion | flops 757334016 | bytes 9633792 | tf_op jit(solution)/shard_map/jrd,jrf->jdf/dot_general | solution.py:90
  172.0 5.9 %convolution_convert_fusion = bf16[16,768,192]{1,2,0:T(8,128)(2,1)} fusion(bf16[16,160,192]{2,1,0:T(8,128)(2,1)S(1)} %get-tuple-element.39, bf16[16,160,1536]{2,1,0:T(8,128)(2,1)} %bitcast.51), kind=kOutput, calls=%fused_computation.17 | convolution fusion | flops 757334016 | bytes 9633792 | tf_op jit(solution)/shard_map/jrd,jrf->jdf/dot_general | solution.py:91
  178.0 3.5 %fusion.8 = bf16[16,192,768]{2,1,0:T(8,128)(2,1)} fusion(bf16[16,160,192]{2,1,0:T(8,128)(2,1)S(1)} %copy-done.2, f32[16,160]{1,0:T(8,128)S(1)} %mul.54, bf16[16,160,1536]{2,1,0:T(8,128)(2,1)S(1)} %bitcast.54), kind=kOutput, calls=%fused_computation.16 | convolution fusion | flops 763232256 | bytes 9977856 | tf_op jit(solution)/shard_map/jrf,jrd->jfd/dot_general | solution.py:93
  181.5 52.0 %reduce-scatter.4.cloned.1.call-done = bf16[128,776]{1,0:T(8,128)(2,1)} async-done(((bf16[1024,776]{1,0:T(8,128)(2,1)}), bf16[128,776]{1,0:T(8,128)(2,1)}) %reduce-scatter.4.cloned.1.call-update) | async-done | bytes 198672
  234.9 1.6 slice.48
  (45 shorter events, 9.4 us)
Async XLA Ops:
  7.2 70.7 %all-gather.2.cloned.1.call-start = ((), (), s32[]{:S(2)}) async-start(), calls=%async_computation.1 | async-start | bytes 3575808 | tf_op jit(solution)/shard_map/all_gather | solution.py:43
  11.6 123.6 %all-reduce.2.cloned.1.call-start = ((), (), s32[]{:S(2)}) async-start(), calls=%async_computation.2 | async-start | bytes 6553600 | tf_op jit(solution)/shard_map/psum | solution.py:61
  78.7 1.9 slice-start.2
  95.5 11.1 %copy-start.1 = (bf16[16,2,80,1536]{3,2,1,0:T(8,128)(2,1)}, bf16[16,2,80,1536]{3,2,1,0:T(8,128)(2,1)S(1)}, u32[]{:S(2)}) copy-start(bf16[16,2,80,1536]{3,2,1,0:T(8,128)(2,1)S(1)} %copy.71) | copy-start | bytes 23592964
  113.4 120.1 %reduce-scatter.4.cloned.1.call-start = ((), (), s32[]{:S(2)}) async-start(), calls=%async_computation.3 | async-start | bytes 2064384
  137.8 3.2 %copy-start = (f32[16,160,576]{2,1,0:T(8,128)}, f32[16,160,576]{2,1,0:T(8,128)S(1)}, u32[]{:S(2)}) copy-start(f32[16,160,576]{2,1,0:T(8,128)S(1)} %convert_element_type.75) | copy-start | bytes 17694724
  143.8 8.3 %slice-start.3 = ((s8[4718592]{0:T(1024)(128)(4,1)}), s8[4194304]{0:T(1024)(128)(4,1)S(1)}, s32[]{:S(2)}) async-start(s8[4718592]{0:T(1024)(128)(4,1)} %bitcast.55), calls=%async_computation.7 | async-start | bytes 8388608
  148.5 3.6 %slice-start.4 = ((s8[4718592]{0:T(1024)(128)(4,1)}), s8[524288]{0:T(1024)(128)(4,1)S(1)}, s32[]{:S(2)}) async-start(s8[4718592]{0:T(1024)(128)(4,1)} %bitcast.55), calls=%async_computation.8 | async-start | bytes 1048576
  166.1 11.9 %slice-start = ((s8[7864320]{0:T(1024)(128)(4,1)}), s8[4194304]{0:T(1024)(128)(4,1)S(1)}, s32[]{:S(2)}) async-start(s8[7864320]{0:T(1024)(128)(4,1)} %bitcast.52), calls=%async_computation.4 | async-start | bytes 8388608
  172.0 5.9 %slice-start.1 = ((s8[7864320]{0:T(1024)(128)(4,1)}), s8[3670016]{0:T(1024)(128)(4,1)S(1)}, s32[]{:S(2)}) async-start(s8[7864320]{0:T(1024)(128)(4,1)} %bitcast.52), calls=%async_computation.5 | async-start | bytes 7340032
  172.0 5.9 %copy-start.2 = (bf16[16,160,192]{2,1,0:T(8,128)(2,1)S(1)}, bf16[16,160,192]{2,1,0:T(8,128)(2,1)}, u32[]{:S(2)}) copy-start(bf16[16,160,192]{2,1,0:T(8,128)(2,1)} %get-tuple-element.38) | copy-start | bytes 2949124
Sparse Core Ops, SparseCore 0:
  11.7 66.1 all-gather.1
  113.5 21.6 all-reduce.1
  166.2 67.2 reduce-scatter.3

commit v2 on v1

--- a/solution.py
+++ b/solution.py
@@ -1,6 +1,10 @@
+import functools
+
 import jax
 import jax.numpy as jnp
 from jax import lax
+from jax.experimental import pallas as pl
+from jax.experimental.pallas import tpu as pltpu
 from jax.sharding import PartitionSpec as P
 
 F32 = jnp.float32
@@ -31,7 +35,7 @@
     return picked.astype(BF16), row_prob, hits, runs, span, rows
 
 
-def on_device(tokens, out_grad, expert_ids, gate_probs, gate_weight, up_weight, down_weight):
+def on_device_wide(tokens, out_grad, expert_ids, gate_probs, gate_weight, up_weight, down_weight):
     tok_rows, width = tokens.shape
     top_count = expert_ids.shape[1]
     per_dev = gate_weight.shape[0]
@@ -100,6 +104,397 @@
     )
 
 
+MESH = pl.DeviceIdType.MESH
+PAD = 16
+TRANS_LHS = (((0,), (0,)), ((), ()))
+TRANS_RHS = (((1,), (1,)), ((), ()))
+
+
+def dot_t(a, b, dims):
+    return lax.dot_general(a, b, dims, preferred_element_type=F32)
+
+
+def route_kernel(
+    owners, run, slots, top_count,
+    tok_in, grad_in, gw_hbm, uw_hbm, dw_hbm,
+    out, xs_hbm, dr_hbm, back_hbm,
+    tok, grd, gw, uw, dw, xs, gs, onehot, prob, part, peer, pair, tp, rx, rz,
+    w_sem, send_z, recv_z, send_x, recv_x, send_i, recv_i, o_sem,
+    send_a, recv_a, send_b, recv_b,
+):
+    m = lax.axis_index("expert")
+    j = lax.axis_index("dp")
+    i = lax.axis_index("inner")
+    blocks, tall, width = tok.shape
+    rows_blk = tall - PAD
+    per_dev, rows, _ = xs.shape
+    hid = gw.shape[2]
+    hid_pad = part.shape[2] // 3
+    runs = blocks // run
+    span = run * rows_blk
+    x_dev, i_dev = {"dp": 1 - j}, {"inner": 1 - i}
+
+    loads = [
+        pltpu.make_async_copy(s, d, w_sem.at[n])
+        for n, (s, d) in enumerate(((gw_hbm, gw), (uw_hbm, uw), (dw_hbm, dw)))
+    ]
+    for load in loads:
+        load.start()
+
+    barrier = pltpu.get_barrier_semaphore()
+    pl.semaphore_signal(barrier, inc=1, device_id=x_dev, device_id_type=MESH)
+    pl.semaphore_signal(barrier, inc=1, device_id=i_dev, device_id_type=MESH)
+    for d in range(1, owners):
+        pl.semaphore_signal(
+            barrier, inc=1, device_id={"expert": lax.rem(m + d, owners)}, device_id_type=MESH
+        )
+    pl.semaphore_wait(barrier, owners + 1)
+
+    bufs = (tok, grd)
+    own = (tok_in, grad_in)
+
+    def hop(c, origin, right, step):
+        block = 2 * origin + j
+        lane = 0 if right else 1
+        return pltpu.make_async_remote_copy(
+            src_ref=own[c] if step == 0 else bufs[c].at[block],
+            dst_ref=bufs[c].at[block],
+            send_sem=send_z.at[c, lane, step],
+            recv_sem=recv_z.at[c, lane, step],
+            device_id={"expert": jnp.clip(m + 1 if right else m - 1, 0, owners - 1)},
+            device_id_type=MESH,
+        )
+
+    def cross(c, origin, block_j, mine):
+        return pltpu.make_async_remote_copy(
+            src_ref=own[c] if mine else bufs[c].at[2 * origin + block_j],
+            dst_ref=bufs[c].at[2 * origin + block_j],
+            send_sem=send_x.at[c, origin],
+            recv_sem=recv_x.at[c, origin],
+            device_id=x_dev,
+            device_id_type=MESH,
+        )
+
+    def can_send(right, origin):
+        if right:
+            return (m + 1 < owners) & (origin >= 0)
+        return (m >= 1) & (origin < owners)
+
+    for c in range(2):
+        cross(c, m, j, True).start()
+        for right in (True, False):
+            @pl.when(can_send(right, m))
+            def _(c=c, right=right):
+                hop(c, m, right, 0).start()
+    tok[2 * m + j] = tok_in[...]
+    grd[2 * m + j] = grad_in[...]
+    for step in range(1, owners):
+        for c in range(2):
+            for right in (True, False):
+                origin = m - step if right else m + step
+
+                @pl.when((origin >= 0) & (origin < owners))
+                def _(c=c, right=right, origin=origin, step=step):
+                    hop(c, origin, right, step - 1).wait_recv()
+                    if step < owners - 1:
+                        @pl.when(can_send(right, origin))
+                        def _():
+                            hop(c, origin, right, step).start()
+                    cross(c, origin, j, False).start()
+
+    at = lax.broadcasted_iota(jnp.int32, (span, span), 0)
+    to = lax.broadcasted_iota(jnp.int32, (span, span), 1)
+    earlier = (at < to).astype(BF16)
+    place = lax.broadcasted_iota(jnp.int32, (slots, span), 0)
+    expert_of = lax.broadcasted_iota(jnp.int32, (per_dev, span), 0) + m * per_dev
+
+    def ids_of(g):
+        return jnp.concatenate(
+            [tok[g * run + b, rows_blk:tall, :rows_blk].astype(F32) for b in range(run)], axis=1
+        )
+
+    for o in range(owners):
+        cross(0, o, 1 - j, False).wait_recv()
+    for g in range(runs):
+        meta = ids_of(g)
+        ids = meta.astype(jnp.int32)
+        member = jnp.zeros((per_dev, span), F32)
+        weight = jnp.zeros((per_dev, span), F32)
+        for k in range(top_count):
+            hit = expert_of == ids[k : k + 1, :]
+            member = member + jnp.where(hit, 1.0, 0.0)
+            weight = weight + jnp.where(hit, meta[top_count + k : top_count + k + 1, :], 0.0)
+        slot = jnp.dot(member.astype(BF16), earlier, preferred_element_type=F32).astype(jnp.int32)
+        slot = jnp.where(member > 0.5, slot, -1)
+        for e in range(per_dev):
+            hit = place == slot[e : e + 1, :]
+            onehot[g, e] = jnp.where(hit, 1.0, 0.0).astype(BF16)
+            prob[e, g * slots : (g + 1) * slots, :] = jnp.sum(
+                jnp.where(hit, weight[e : e + 1, :], 0.0), axis=1, keepdims=True
+            )
+
+    batch = 4 if per_dev % 4 == 0 else 1
+
+    def spread(buf, dest):
+        for g in range(runs):
+            whole = buf[g * run : (g + 1) * run, :rows_blk, :].reshape(span, width)
+
+            @pl.loop(0, per_dev // batch)
+            def _(n):
+                pick = onehot[g, pl.ds(n * batch, batch)].reshape(batch * slots, span)
+                got = jnp.dot(pick, whole, preferred_element_type=F32).astype(BF16)
+                dest[pl.ds(n * batch, batch), g * slots : (g + 1) * slots, :] = got.reshape(
+                    batch, slots, width
+                )
+
+    spread(tok, xs)
+    for load in loads:
+        load.wait()
+    xs_out = pltpu.make_async_copy(xs, xs_hbm, o_sem.at[2, 0])
+    xs_out.start()
+
+    @pl.loop(0, per_dev)
+    def _(e):
+        rows_e = xs[e]
+        part[e, :, 0:hid] = jnp.dot(rows_e, gw[e], preferred_element_type=F32).astype(BF16)
+        part[e, :, hid_pad : hid_pad + hid] = jnp.dot(
+            rows_e, uw[e], preferred_element_type=F32
+        ).astype(BF16)
+
+    for o in range(owners):
+        cross(1, o, 1 - j, False).wait_recv()
+    spread(grd, gs)
+
+    def swap(e):
+        return pltpu.make_async_remote_copy(
+            src_ref=part.at[e], dst_ref=peer.at[e],
+            send_sem=send_i.at[e], recv_sem=recv_i.at[e],
+            device_id=i_dev, device_id_type=MESH,
+        )
+
+    @pl.loop(0, per_dev)
+    def _(e):
+        part[e, :, 2 * hid_pad : 2 * hid_pad + hid] = dot_t(gs[e], dw[e], TRANS_RHS).astype(BF16)
+        swap(e).start()
+
+    pair[...] = jnp.zeros_like(pair)
+
+    def back_out(e):
+        return pltpu.make_async_copy(part.at[e], back_hbm.at[e], o_sem.at[0, e])
+
+    def rows_out(e):
+        return pltpu.make_async_copy(gs.at[e], dr_hbm.at[e], o_sem.at[1, e])
+
+    @pl.loop(0, per_dev)
+    def _(e):
+        swap(e).wait()
+
+        def total(n):
+            cols = slice(n * hid_pad, n * hid_pad + hid)
+            return part[e, :, cols].astype(F32) + peer[e, :, cols].astype(F32)
+
+        gate, up, slope = total(0), total(1), total(2)
+        col = prob[e]
+        sig = jax.nn.sigmoid(gate)
+        act = gate * sig
+        hidden = (act * up).astype(BF16)
+        score = jnp.sum(hidden.astype(F32) * slope, axis=1, keepdims=True)
+        hidden_grad = col * slope
+        gate_back = (hidden_grad * up * sig * (1.0 + gate * (1.0 - sig))).astype(BF16)
+        up_back = (hidden_grad * act).astype(BF16)
+        part[e, :, 0:hid] = gate_back
+        part[e, :, hid_pad : hid_pad + hid] = up_back
+        part[e, :, 2 * hid_pad : 2 * hid_pad + hid] = hidden
+        back_out(e).start()
+        gs[e] = (col * gs[e].astype(F32)).astype(BF16)
+        rows_out(e).start()
+        peer[e] = (dot_t(gate_back, gw[e], TRANS_RHS) + dot_t(up_back, uw[e], TRANS_RHS)).astype(
+            BF16
+        )
+        for g in range(runs):
+            ids = ids_of(g)[:top_count, :].astype(jnp.int32)
+            seen = jnp.sum(
+                onehot[g, e].astype(F32) * score[g * slots : (g + 1) * slots, :],
+                axis=0, keepdims=True,
+            )
+            pair[g] += jnp.where(ids == m * per_dev + e, seen, 0.0)
+
+    def give(o):
+        return pltpu.make_async_remote_copy(
+            src_ref=tp.at[2 * o + 1 - j], dst_ref=rx.at[o],
+            send_sem=send_a.at[o], recv_sem=recv_a.at[o],
+            device_id=x_dev, device_id_type=MESH,
+        )
+
+    def deliver(o, slot_at):
+        return pltpu.make_async_remote_copy(
+            src_ref=tp.at[2 * o + j], dst_ref=rz.at[slot_at],
+            send_sem=send_b.at[o], recv_sem=recv_b.at[slot_at],
+            device_id={"expert": o}, device_id_type=MESH,
+        )
+
+    for g in range(runs):
+        back = peer[:, g * slots : (g + 1) * slots, :].reshape(per_dev * slots, width)
+        pick = onehot[g].reshape(per_dev * slots, span)
+        for b in range(run):
+            n = g * run + b
+            cols = slice(b * rows_blk, (b + 1) * rows_blk)
+            tp[n, 0:rows_blk, :] = dot_t(pick[:, cols], back, TRANS_LHS).astype(BF16)
+            tp[n, rows_blk:tall, :] = jnp.zeros((PAD, width), BF16)
+            tp[n, rows_blk:tall, 0:rows_blk] = jnp.concatenate(
+                [pair[g, :, cols], jnp.zeros((PAD - top_count, rows_blk), F32)], axis=0
+            ).astype(BF16)
+            if n % 2 == 1:
+                give(n // 2).start()
+
+    for o in range(owners):
+        give(o).wait_recv()
+
+        @pl.when(o != m)
+        def _(o=o):
+            tp[2 * o + j] = (tp[2 * o + j].astype(F32) + rx[o].astype(F32)).astype(BF16)
+            deliver(o, m).start()
+
+    acc = tp[2 * m + j].astype(F32) + rx[m].astype(F32)
+    out[...] = acc
+    for o in range(owners):
+        @pl.when(o != m)
+        def _(o=o):
+            deliver(o, o).wait_recv()
+            out[...] += rz[o].astype(F32)
+
+    for o in range(owners):
+        give(o).wait_send()
+
+        @pl.when(o != m)
+        def _(o=o):
+            deliver(o, o).wait_send()
+        for c in range(2):
+            cross(c, o, j, False).wait_send()
+    for step in range(owners - 1):
+        for c in range(2):
+            for right in (True, False):
+                origin = m - step if right else m + step
+
+                @pl.when(can_send(right, origin))
+                def _(c=c, right=right, origin=origin, step=step):
+                    hop(c, origin, right, step).wait_send()
+    xs_out.wait()
+
+    @pl.loop(0, per_dev)
+    def _(e):
+        back_out(e).wait()
+        rows_out(e).wait()
+
+
+def weights_kernel(hid, hid_pad, xs, dr, back, gate_out, up_out, down_out):
+    rows_e = xs[0]
+    gate_out[0] = dot_t(rows_e, back[0, :, 0:hid], TRANS_LHS).astype(BF16)
+    up_out[0] = dot_t(rows_e, back[0, :, hid_pad : hid_pad + hid], TRANS_LHS).astype(BF16)
+    down_out[0] = dot_t(back[0, :, 2 * hid_pad : 2 * hid_pad + hid], dr[0], TRANS_LHS).astype(BF16)
+
+
+def on_device(tokens, out_grad, expert_ids, gate_probs, gate_weight, up_weight, down_weight):
+    args = (tokens, out_grad, expert_ids, gate_probs, gate_weight, up_weight, down_weight)
+    tok_rows, width = tokens.shape
+    top_count = expert_ids.shape[1]
+    per_dev, _, hid = gate_weight.shape
+    owners = lax.axis_size("expert")
+    blocks = owners * lax.axis_size("dp")
+    capacity = tok_rows * top_count // (per_dev * owners) + 1
+    run = 4 if blocks % 4 == 0 else 2
+    runs = blocks // run
+    slots = -(-run * capacity // 16) * 16
+    rows = runs * slots
+    hid_pad = -(-hid // 128) * 128
+    tall = tok_rows + PAD
+    scratch = [
+        ((blocks, tall, width), BF16),
+        ((blocks, tok_rows, width), BF16),
+        (gate_weight.shape, BF16),
+        (up_weight.shape, BF16),
+        (down_weight.shape, BF16),
+        ((per_dev, rows, width), BF16),
+        ((per_dev, rows, width), BF16),
+        ((runs, per_dev, slots, run * tok_rows), BF16),
+        ((per_dev, rows, 1), F32),
+        ((per_dev, rows, 3 * hid_pad), BF16),
+        ((per_dev, rows, width), BF16),
+        ((runs, top_count, run * tok_rows), F32),
+        ((blocks, tall, width), BF16),
+        ((owners, tall, width), BF16),
+        ((owners, tall, width), BF16),
+    ]
+    need = 0
+    for shape, dtype in scratch:
+        lanes = -(-shape[-1] // 128) * 128
+        size = lanes * (2 if dtype == BF16 else 4)
+        for n in shape[:-1]:
+            size *= n
+        need += size
+    fits = need < 54 * 2**20 and lax.axis_size("dp") == 2 and lax.axis_size("inner") == 2
+    fits = fits and tok_rows == 128 and top_count == 8 and 3 * hid_pad == width
+    if not fits:
+        return on_device_wide(*args)
+    meta = jnp.concatenate([expert_ids.astype(BF16).T, gate_probs.astype(BF16).T], axis=0)
+    tok_in = jnp.concatenate([tokens, jnp.pad(meta, ((0, 0), (0, width - tok_rows)))], axis=0)
+    vmem = pl.BlockSpec(memory_space=pltpu.VMEM)
+    hbm = pl.BlockSpec(memory_space=pl.ANY)
+    dma = pltpu.SemaphoreType.DMA
+    out, xs, dr, back = pl.pallas_call(
+        functools.partial(route_kernel, owners, run, slots, top_count),
+        out_shape=(
+            jax.ShapeDtypeStruct((tall, width), F32),
+            jax.ShapeDtypeStruct((per_dev, rows, width), BF16),
+            jax.ShapeDtypeStruct((per_dev, rows, width), BF16),
+            jax.ShapeDtypeStruct((per_dev, rows, 3 * hid_pad), BF16),
+        ),
+        in_specs=[vmem, vmem, hbm, hbm, hbm],
+        out_specs=(vmem, hbm, hbm, hbm),
+        scratch_shapes=[pltpu.VMEM(shape, dtype) for shape, dtype in scratch]
+        + [
+            dma((3,)),
+            dma((2, 2, owners)),
+            dma((2, 2, owners)),
+            dma((2, owners)),
+            dma((2, owners)),
+            dma((per_dev,)),
+            dma((per_dev,)),
+            dma((3, per_dev)),
+            dma((owners,)),
+            dma((owners,)),
+            dma((owners,)),
+            dma((owners,)),
+        ],
+        compiler_params=pltpu.CompilerParams(
+            collective_id=0, has_side_effects=True, vmem_limit_bytes=62 * 2**20
+        ),
+        name="route",
+    )(tok_in, out_grad, gate_weight, up_weight, down_weight)
+
+    def one(a, b):
+        return pl.BlockSpec((1, a, b), lambda e: (e, 0, 0))
+
+    grads = pl.pallas_call(
+        functools.partial(weights_kernel, hid, hid_pad),
+        grid=(per_dev,),
+        out_shape=(
+            jax.ShapeDtypeStruct(gate_weight.shape, BF16),
+            jax.ShapeDtypeStruct(up_weight.shape, BF16),
+            jax.ShapeDtypeStruct(down_weight.shape, BF16),
+        ),
+        in_specs=[one(rows, width), one(rows, width), one(rows, 3 * hid_pad)],
+        out_specs=(one(width, hid), one(width, hid), one(hid, width)),
+        compiler_params=pltpu.CompilerParams(vmem_limit_bytes=32 * 2**20),
+        name="weight_grads",
+    )(xs, dr, back)
+    return (
+        out[:tok_rows].astype(BF16),
+        out[tok_rows : tok_rows + top_count, :tok_rows].T,
+        *grads,
+    )
+
+
 def solution(mesh):
     placed = (
         P(("groups", "expert", "dp"), "inner"),

time: 244 us -> 156 us (0.64)
  the two profiles are of different devices: /device:TPU:0 before, /device:TPU:26 now
where the time goes in v2:
time: 156 us; the launch traced here: 155 us
  Pallas kernels  107 us (69%)
  local copies, waits for them, and re-layouts  43.8 us (28%)
  other arithmetic  3.01 us (2%)
    pallas_call x1, Pallas kernels, on_device(): pl.pallas_call(functools.partial(route_kernel, owners, run, slots, top_co...  96.6 us
    unnamed x12, local copies, waits for them, and re-layouts  40.8 us
    pallas_call x1, Pallas kernels, on_device(): pl.pallas_call(functools.partial(weights_kernel, hid, hid_pad), grid=(per...  10.6 us

profile of v2, /device:TPU:26, one launch (start us, length us, event | category | flops | bytes accessed | tf_op | source)
XLA Modules:
  0.0 154.6 jit_solution(5326063587174082555)
XLA Ops:
  0.6 0.7 convert_bitcast_fusion.1
  1.3 0.7 convert_bitcast_fusion
  2.0 1.6 %pad_maximum_fusion.tok_in = bf16[144,768]{1,0:T(8,128)(2,1)} fusion(bf16[16,768]{1,0:T(8,128)(2,1)S(1)} %fusion.2, bf16[128,768]{1,0:T(8,128)(2,1)} %param.7), kind=kLoop, calls=%fused_computation.1 | loop fusion | flops 442368 | bytes 442368 | tf_op jit(solution)/shard_map/concatenate | solution.py:440
  3.6 7.9 %copy.12.gw_hbm = bf16[16,768,192]{2,1,0:T(8,128)(2,1)} copy(bf16[16,768,192]{1,2,0:T(8,128)(2,1)} %param.11) | data formatting | bytes 9437184 | tf_op args[4]
  11.6 8.0 %copy.13.uw_hbm = bf16[16,768,192]{2,1,0:T(8,128)(2,1)} copy(bf16[16,768,192]{1,2,0:T(8,128)(2,1)} %param.12) | data formatting | bytes 9437184 | tf_op args[5]
  19.6 96.6 %route.1 = (f32[144,768]{1,0:T(8,128)}, bf16[16,160,768]{2,1,0:T(8,128)(2,1)}, bf16[16,160,768]{2,1,0:T(8,128)(2,1)}, bf16[16,160,768]{2,1,0:T(8,128)(2,1)}) custom-call(bf16[144,768]{1,0:T(8,128)(2,1)} %pad_maximum_fusion.tok_in, bf16[128,768]{1,0:T(8,128)(2,1)} %grad_in.1, bf16[16,768,192]{2,1,0:T(8,128)(2,1)} %copy.12.gw_hbm, ...), custom_call_target="tpu_custom_call" | custom-call | tf_op jit(solution)/shard_map/route/pallas_call | solution.py:444
  116.1 1.3 slice_bitcast_fusion
  117.4 1.7 %slice.12 = bf16[128,768]{1,0:T(8,128)(2,1)} slice(f32[144,768]{1,0:T(8,128)} %get-tuple-element.12), slice={[0:128], [0:768]} | slice | bytes 393216 | tf_op jit(solution)/shard_map/slice | solution.py:492
  119.1 0.0 copy-start.1
  119.1 2.1 %copy-done.1 = bf16[16,160,768]{2,1,0:T(8,128)(2,1)S(1)} copy-done((bf16[16,160,768]{2,1,0:T(8,128)(2,1)S(1)}, bf16[16,160,768]{2,1,0:T(8,128)(2,1)}, u32[]{:S(2)}) %copy-start.1) | copy-done | bytes 3932184
  121.2 0.0 copy-start.2
  121.2 2.1 %copy-done.2 = bf16[16,160,768]{2,1,0:T(8,128)(2,1)S(1)} copy-done((bf16[16,160,768]{2,1,0:T(8,128)(2,1)S(1)}, bf16[16,160,768]{2,1,0:T(8,128)(2,1)}, u32[]{:S(2)}) %copy-start.2) | copy-done | bytes 3932184
  123.3 0.0 copy-start.3
  123.3 2.1 %copy-done.3 = bf16[16,160,768]{2,1,0:T(8,128)(2,1)S(1)} copy-done((bf16[16,160,768]{2,1,0:T(8,128)(2,1)S(1)}, bf16[16,160,768]{2,1,0:T(8,128)(2,1)}, u32[]{:S(2)}) %copy-start.3) | copy-done | bytes 3932184
  125.4 10.6 %weight_grads.1 = (bf16[16,768,192]{2,1,0:T(8,128)(2,1)S(1)}, bf16[16,768,192]{2,1,0:T(8,128)(2,1)}, bf16[16,192,768]{2,1,0:T(8,128)(2,1)}) custom-call(bf16[16,160,768]{2,1,0:T(8,128)(2,1)S(1)} %copy-done.1, bf16[16,160,768]{2,1,0:T(8,128)(2,1)S(1)} %copy-done.2, bf16[16,160,768]{2,1,0:T(8,128)(2,1)S(1)} %copy-done.3), custom_call_target="tpu_custom_call" | custom-call | tf_op jit(solution)/shard_map/weight_grads/pallas_call | solution.py:478
  136.0 0.0 copy-start
  136.0 2.6 %copy-done = bf16[16,768,192]{2,1,0:T(8,128)(2,1)} copy-done((bf16[16,768,192]{2,1,0:T(8,128)(2,1)}, bf16[16,768,192]{2,1,0:T(8,128)(2,1)S(1)}, u32[]{:S(2)}) %copy-start) | copy-done | bytes 4718616
  138.7 8.0 %copy.14 = bf16[16,768,192]{1,2,0:T(8,128)(2,1)} copy(bf16[16,768,192]{2,1,0:T(8,128)(2,1)} %copy-done) | data formatting | bytes 9437184
  146.6 8.0 %copy.15 = bf16[16,768,192]{1,2,0:T(8,128)(2,1)} copy(bf16[16,768,192]{2,1,0:T(8,128)(2,1)} %get-tuple-element.22) | data formatting | bytes 9437184
  (1 shorter events, 0.0 us)
Async XLA Ops:
  119.1 2.1 %copy-start.1 = (bf16[16,160,768]{2,1,0:T(8,128)(2,1)S(1)}, bf16[16,160,768]{2,1,0:T(8,128)(2,1)}, u32[]{:S(2)}) copy-start(bf16[16,160,768]{2,1,0:T(8,128)(2,1)} %get-tuple-element.13.xs) | copy-start | bytes 11796484
  121.2 2.1 %copy-start.2 = (bf16[16,160,768]{2,1,0:T(8,128)(2,1)S(1)}, bf16[16,160,768]{2,1,0:T(8,128)(2,1)}, u32[]{:S(2)}) copy-start(bf16[16,160,768]{2,1,0:T(8,128)(2,1)} %get-tuple-element.14.dr) | copy-start | bytes 11796484
  123.3 2.1 %copy-start.3 = (bf16[16,160,768]{2,1,0:T(8,128)(2,1)S(1)}, bf16[16,160,768]{2,1,0:T(8,128)(2,1)}, u32[]{:S(2)}) copy-start(bf16[16,160,768]{2,1,0:T(8,128)(2,1)} %get-tuple-element.15.back) | copy-start | bytes 11796484
  136.0 2.6 %copy-start = (bf16[16,768,192]{2,1,0:T(8,128)(2,1)}, bf16[16,768,192]{2,1,0:T(8,128)(2,1)S(1)}, u32[]{:S(2)}) copy-start(bf16[16,768,192]{2,1,0:T(8,128)(2,1)S(1)} %get-tuple-element.21) | copy-start | bytes 14155780

commit v3 on v2

--- a/solution.py
+++ b/solution.py
@@ -117,9 +117,10 @@
 def route_kernel(
     owners, run, slots, top_count,
     tok_in, grad_in, gw_hbm, uw_hbm, dw_hbm,
-    out, xs_hbm, dr_hbm, back_hbm,
-    tok, grd, gw, uw, dw, xs, gs, onehot, prob, part, peer, pair, tp, rx, rz,
-    w_sem, send_z, recv_z, send_x, recv_x, send_i, recv_i, o_sem,
+    out, xs_hbm, gs_hbm, back_hbm,
+    tok, grd, gw, uw, dw, xs, gs, onehot, prob, part, peer, part_s, peer_s, back, rowg,
+    pair, chosen, tp, rx, rz,
+    w_sem, send_z, recv_z, send_x, recv_x, send_i, recv_i, send_s, recv_s, o_sem,
     send_a, recv_a, send_b, recv_b,
 ):
     m = lax.axis_index("expert")
@@ -128,8 +129,8 @@
     blocks, tall, width = tok.shape
     rows_blk = tall - PAD
     per_dev, rows, _ = xs.shape
-    hid = gw.shape[2]
-    hid_pad = part.shape[2] // 3
+    hid = gw.shape[1]
+    hid_pad = part_s.shape[2]
     runs = blocks // run
     span = run * rows_blk
     x_dev, i_dev = {"dp": 1 - j}, {"inner": 1 - i}
@@ -180,27 +181,38 @@
             return (m + 1 < owners) & (origin >= 0)
         return (m >= 1) & (origin < owners)
 
-    for c in range(2):
-        cross(c, m, j, True).start()
+    def begin(c):
         for right in (True, False):
             @pl.when(can_send(right, m))
-            def _(c=c, right=right):
+            def _(right=right):
                 hop(c, m, right, 0).start()
+        cross(c, m, j, True).start()
+
+    def advance(c, step):
+        for right in (True, False):
+            origin = m - step if right else m + step
+
+            @pl.when((origin >= 0) & (origin < owners))
+            def _(right=right, origin=origin):
+                hop(c, origin, right, step - 1).wait_recv()
+                if step < owners - 1:
+                    @pl.when(can_send(right, origin))
+                    def _():
+                        hop(c, origin, right, step).start()
+                cross(c, origin, j, False).start()
+
+    begin(0)
     tok[2 * m + j] = tok_in[...]
+    for step in range(1, owners):
+        advance(0, step)
+        if step == max(1, owners - 2):
+            begin(1)
     grd[2 * m + j] = grad_in[...]
-    for step in range(1, owners):
-        for c in range(2):
-            for right in (True, False):
-                origin = m - step if right else m + step
-
-                @pl.when((origin >= 0) & (origin < owners))
-                def _(c=c, right=right, origin=origin, step=step):
-                    hop(c, origin, right, step - 1).wait_recv()
-                    if step < owners - 1:
-                        @pl.when(can_send(right, origin))
-                        def _():
-                            hop(c, origin, right, step).start()
-                    cross(c, origin, j, False).start()
+    pending = list(range(1, owners))
+
+    def advance_next():
+        if pending:
+            advance(1, pending.pop(0))
 
     at = lax.broadcasted_iota(jnp.int32, (span, span), 0)
     to = lax.broadcasted_iota(jnp.int32, (span, span), 1)
@@ -226,12 +238,14 @@
             weight = weight + jnp.where(hit, meta[top_count + k : top_count + k + 1, :], 0.0)
         slot = jnp.dot(member.astype(BF16), earlier, preferred_element_type=F32).astype(jnp.int32)
         slot = jnp.where(member > 0.5, slot, -1)
+        chosen[g] = ids[:top_count, :]
         for e in range(per_dev):
             hit = place == slot[e : e + 1, :]
             onehot[g, e] = jnp.where(hit, 1.0, 0.0).astype(BF16)
             prob[e, g * slots : (g + 1) * slots, :] = jnp.sum(
                 jnp.where(hit, weight[e : e + 1, :], 0.0), axis=1, keepdims=True
             )
+        advance_next()
 
     batch = 4 if per_dev % 4 == 0 else 1
 
@@ -248,22 +262,12 @@
                 )
 
     spread(tok, xs)
+    xs_out = pltpu.make_async_copy(xs, xs_hbm, o_sem.at[1, 0])
+    xs_out.start()
+    while pending:
+        advance_next()
     for load in loads:
         load.wait()
-    xs_out = pltpu.make_async_copy(xs, xs_hbm, o_sem.at[2, 0])
-    xs_out.start()
-
-    @pl.loop(0, per_dev)
-    def _(e):
-        rows_e = xs[e]
-        part[e, :, 0:hid] = jnp.dot(rows_e, gw[e], preferred_element_type=F32).astype(BF16)
-        part[e, :, hid_pad : hid_pad + hid] = jnp.dot(
-            rows_e, uw[e], preferred_element_type=F32
-        ).astype(BF16)
-
-    for o in range(owners):
-        cross(1, o, 1 - j, False).wait_recv()
-    spread(grd, gs)
 
     def swap(e):
         return pltpu.make_async_remote_copy(
@@ -272,52 +276,69 @@
             device_id=i_dev, device_id_type=MESH,
         )
 
+    def swap_s(e):
+        return pltpu.make_async_remote_copy(
+            src_ref=part_s.at[e], dst_ref=peer_s.at[e],
+            send_sem=send_s.at[e], recv_sem=recv_s.at[e],
+            device_id=i_dev, device_id_type=MESH,
+        )
+
     @pl.loop(0, per_dev)
     def _(e):
-        part[e, :, 2 * hid_pad : 2 * hid_pad + hid] = dot_t(gs[e], dw[e], TRANS_RHS).astype(BF16)
+        rows_e = xs[e]
+        part[e, :, 0:hid] = dot_t(rows_e, gw[e], TRANS_RHS).astype(BF16)
+        part[e, :, hid_pad : hid_pad + hid] = dot_t(rows_e, uw[e], TRANS_RHS).astype(BF16)
         swap(e).start()
 
+    for o in range(owners):
+        cross(1, o, 1 - j, False).wait_recv()
+    spread(grd, gs)
+    gs_out = pltpu.make_async_copy(gs, gs_hbm, o_sem.at[1, 1])
+    gs_out.start()
+
+    @pl.loop(0, per_dev)
+    def _(e):
+        part_s[e, :, 0:hid] = dot_t(gs[e], dw[e], TRANS_RHS).astype(BF16)
+        swap_s(e).start()
+
     pair[...] = jnp.zeros_like(pair)
 
     def back_out(e):
-        return pltpu.make_async_copy(part.at[e], back_hbm.at[e], o_sem.at[0, e])
-
-    def rows_out(e):
-        return pltpu.make_async_copy(gs.at[e], dr_hbm.at[e], o_sem.at[1, e])
+        return pltpu.make_async_copy(back.at[e], back_hbm.at[e], o_sem.at[0, e])
 
     @pl.loop(0, per_dev)
     def _(e):
         swap(e).wait()
-
-        def total(n):
+        swap_s(e).wait()
+
+        def total(mine, theirs, n):
             cols = slice(n * hid_pad, n * hid_pad + hid)
-            return part[e, :, cols].astype(F32) + peer[e, :, cols].astype(F32)
-
-        gate, up, slope = total(0), total(1), total(2)
+            return mine[e, :, cols].astype(F32) + theirs[e, :, cols].astype(F32)
+
+        gate, up = total(part, peer, 0), total(part, peer, 1)
+        slope = total(part_s, peer_s, 0)
         col = prob[e]
         sig = jax.nn.sigmoid(gate)
         act = gate * sig
-        hidden = (act * up).astype(BF16)
-        score = jnp.sum(hidden.astype(F32) * slope, axis=1, keepdims=True)
+        hidden = (act * up).astype(BF16).astype(F32)
+        score = jnp.sum(hidden * slope, axis=1, keepdims=True)
         hidden_grad = col * slope
         gate_back = (hidden_grad * up * sig * (1.0 + gate * (1.0 - sig))).astype(BF16)
         up_back = (hidden_grad * act).astype(BF16)
-        part[e, :, 0:hid] = gate_back
-        part[e, :, hid_pad : hid_pad + hid] = up_back
-        part[e, :, 2 * hid_pad : 2 * hid_pad + hid] = hidden
+        back[e, :, 0:hid] = gate_back
+        back[e, :, hid_pad : hid_pad + hid] = up_back
+        back[e, :, 2 * hid_pad : 2 * hid_pad + hid] = (col * hidden).astype(BF16)
         back_out(e).start()
-        gs[e] = (col * gs[e].astype(F32)).astype(BF16)
-        rows_out(e).start()
-        peer[e] = (dot_t(gate_back, gw[e], TRANS_RHS) + dot_t(up_back, uw[e], TRANS_RHS)).astype(
-            BF16
-        )
+        rowg[e] = (
+            jnp.dot(gate_back, gw[e], preferred_element_type=F32)
+            + jnp.dot(up_back, uw[e], preferred_element_type=F32)
+        ).astype(BF16)
         for g in range(runs):
-            ids = ids_of(g)[:top_count, :].astype(jnp.int32)
             seen = jnp.sum(
                 onehot[g, e].astype(F32) * score[g * slots : (g + 1) * slots, :],
                 axis=0, keepdims=True,
             )
-            pair[g] += jnp.where(ids == m * per_dev + e, seen, 0.0)
+            pair[g] += jnp.where(chosen[g] == m * per_dev + e, seen, 0.0)
 
     def give(o):
         return pltpu.make_async_remote_copy(
@@ -333,35 +354,42 @@
             device_id={"expert": o}, device_id_type=MESH,
         )
 
-    for g in range(runs):
-        back = peer[:, g * slots : (g + 1) * slots, :].reshape(per_dev * slots, width)
-        pick = onehot[g].reshape(per_dev * slots, span)
-        for b in range(run):
-            n = g * run + b
-            cols = slice(b * rows_blk, (b + 1) * rows_blk)
-            tp[n, 0:rows_blk, :] = dot_t(pick[:, cols], back, TRANS_LHS).astype(BF16)
-            tp[n, rows_blk:tall, :] = jnp.zeros((PAD, width), BF16)
-            tp[n, rows_blk:tall, 0:rows_blk] = jnp.concatenate(
-                [pair[g, :, cols], jnp.zeros((PAD - top_count, rows_blk), F32)], axis=0
-            ).astype(BF16)
-            if n % 2 == 1:
-                give(n // 2).start()
-
-    for o in range(owners):
+    order = []
+    for k in range(owners):
+        found, at_k = m * 0, m * 0
+        for d in range(owners - 1, -1, -1):
+            for cand in (m + d, m - d) if d else (m,):
+                valid = (cand >= 0) & (cand < owners)
+                at_k = jnp.where(valid & (found == k), cand, at_k)
+                found = found + jnp.where(valid, 1, 0)
+        order.append(at_k)
+
+    def combine(n):
+        g, b = n // run, n % run
+        rows_at = pl.ds(pl.multiple_of(g * slots, 16), slots)
+        cols = pl.ds(pl.multiple_of(b * rows_blk, 128), rows_blk)
+        mine = rowg[:, rows_at, :].reshape(per_dev * slots, width)
+        pick = onehot[g, :, :, cols].reshape(per_dev * slots, rows_blk)
+        tp[n, 0:rows_blk, :] = dot_t(pick, mine, TRANS_LHS).astype(BF16)
+        tp[n, rows_blk:tall, :] = jnp.zeros((PAD, width), BF16)
+        tp[n, rows_blk:tall, 0:rows_blk] = jnp.concatenate(
+            [pair[g, :, cols], jnp.zeros((PAD - top_count, rows_blk), F32)], axis=0
+        ).astype(BF16)
+
+    for o in order:
+        combine(2 * o + 1 - j)
+        give(o).start()
+    for k, o in enumerate(order):
+        combine(2 * o + j)
         give(o).wait_recv()
-
-        @pl.when(o != m)
-        def _(o=o):
+        if k < owners - 1:
             tp[2 * o + j] = (tp[2 * o + j].astype(F32) + rx[o].astype(F32)).astype(BF16)
             deliver(o, m).start()
-
-    acc = tp[2 * m + j].astype(F32) + rx[m].astype(F32)
-    out[...] = acc
-    for o in range(owners):
-        @pl.when(o != m)
-        def _(o=o):
-            deliver(o, o).wait_recv()
-            out[...] += rz[o].astype(F32)
+        else:
+            out[...] = tp[2 * o + j].astype(F32) + rx[o].astype(F32)
+    for o in order[:-1]:
+        deliver(o, o).wait_recv()
+        out[...] += rz[o].astype(F32)
 
     for o in range(owners):
         give(o).wait_send()
@@ -380,18 +408,18 @@
                 def _(c=c, right=right, origin=origin, step=step):
                     hop(c, origin, right, step).wait_send()
     xs_out.wait()
+    gs_out.wait()
 
     @pl.loop(0, per_dev)
     def _(e):
         back_out(e).wait()
-        rows_out(e).wait()
-
-
-def weights_kernel(hid, hid_pad, xs, dr, back, gate_out, up_out, down_out):
+
+
+def weights_kernel(hid, hid_pad, xs, gs, back, gate_out, up_out, down_out):
     rows_e = xs[0]
-    gate_out[0] = dot_t(rows_e, back[0, :, 0:hid], TRANS_LHS).astype(BF16)
-    up_out[0] = dot_t(rows_e, back[0, :, hid_pad : hid_pad + hid], TRANS_LHS).astype(BF16)
-    down_out[0] = dot_t(back[0, :, 2 * hid_pad : 2 * hid_pad + hid], dr[0], TRANS_LHS).astype(BF16)
+    gate_out[0] = dot_t(back[0, :, 0:hid], rows_e, TRANS_LHS).astype(BF16)
+    up_out[0] = dot_t(back[0, :, hid_pad : hid_pad + hid], rows_e, TRANS_LHS).astype(BF16)
+    down_out[0] = dot_t(back[0, :, 2 * hid_pad : 2 * hid_pad + hid], gs[0], TRANS_LHS).astype(BF16)
 
 
 def on_device(tokens, out_grad, expert_ids, gate_probs, gate_weight, up_weight, down_weight):
@@ -411,16 +439,21 @@
     scratch = [
         ((blocks, tall, width), BF16),
         ((blocks, tok_rows, width), BF16),
-        (gate_weight.shape, BF16),
-        (up_weight.shape, BF16),
+        (down_weight.shape, BF16),
+        (down_weight.shape, BF16),
         (down_weight.shape, BF16),
         ((per_dev, rows, width), BF16),
         ((per_dev, rows, width), BF16),
         ((runs, per_dev, slots, run * tok_rows), BF16),
         ((per_dev, rows, 1), F32),
+        ((per_dev, rows, 2 * hid_pad), BF16),
+        ((per_dev, rows, 2 * hid_pad), BF16),
+        ((per_dev, rows, hid_pad), BF16),
+        ((per_dev, rows, hid_pad), BF16),
         ((per_dev, rows, 3 * hid_pad), BF16),
         ((per_dev, rows, width), BF16),
         ((runs, top_count, run * tok_rows), F32),
+        ((runs, top_count, run * tok_rows), jnp.int32),
         ((blocks, tall, width), BF16),
         ((owners, tall, width), BF16),
         ((owners, tall, width), BF16),
@@ -432,8 +465,8 @@
         for n in shape[:-1]:
             size *= n
         need += size
-    fits = need < 54 * 2**20 and lax.axis_size("dp") == 2 and lax.axis_size("inner") == 2
-    fits = fits and tok_rows == 128 and top_count == 8 and 3 * hid_pad == width
+    fits = need < 57 * 2**20 and lax.axis_size("dp") == 2 and lax.axis_size("inner") == 2
+    fits = fits and owners > 1 and tok_rows == 128 and top_count == 8
     if not fits:
         return on_device_wide(*args)
     meta = jnp.concatenate([expert_ids.astype(BF16).T, gate_probs.astype(BF16).T], axis=0)
@@ -441,7 +474,7 @@
     vmem = pl.BlockSpec(memory_space=pltpu.VMEM)
     hbm = pl.BlockSpec(memory_space=pl.ANY)
     dma = pltpu.SemaphoreType.DMA
-    out, xs, dr, back = pl.pallas_call(
+    out, xs, gs, back = pl.pallas_call(
         functools.partial(route_kernel, owners, run, slots, top_count),
         out_shape=(
             jax.ShapeDtypeStruct((tall, width), F32),
@@ -460,7 +493,9 @@
             dma((2, owners)),
             dma((per_dev,)),
             dma((per_dev,)),
-            dma((3, per_dev)),
+            dma((per_dev,)),
+            dma((per_dev,)),
+            dma((2, max(per_dev, 2))),
             dma((owners,)),
             dma((owners,)),
             dma((owners,)),
@@ -470,28 +505,26 @@
             collective_id=0, has_side_effects=True, vmem_limit_bytes=62 * 2**20
         ),
         name="route",
-    )(tok_in, out_grad, gate_weight, up_weight, down_weight)
+    )(tok_in, out_grad, gate_weight.transpose(0, 2, 1), up_weight.transpose(0, 2, 1), down_weight)
 
     def one(a, b):
         return pl.BlockSpec((1, a, b), lambda e: (e, 0, 0))
 
-    grads = pl.pallas_call(
+    grad_gate, grad_up, grad_down = pl.pallas_call(
         functools.partial(weights_kernel, hid, hid_pad),
         grid=(per_dev,),
-        out_shape=(
-            jax.ShapeDtypeStruct(gate_weight.shape, BF16),
-            jax.ShapeDtypeStruct(up_weight.shape, BF16),
-            jax.ShapeDtypeStruct(down_weight.shape, BF16),
-        ),
+        out_shape=(jax.ShapeDtypeStruct(down_weight.shape, BF16),) * 3,
         in_specs=[one(rows, width), one(rows, width), one(rows, 3 * hid_pad)],
-        out_specs=(one(width, hid), one(width, hid), one(hid, width)),
-        compiler_params=pltpu.CompilerParams(vmem_limit_bytes=32 * 2**20),
+        out_specs=(one(hid, width),) * 3,
+        compiler_params=pltpu.CompilerParams(vmem_limit_bytes=60 * 2**20),
         name="weight_grads",
-    )(xs, dr, back)
+    )(xs, gs, back)
     return (
         out[:tok_rows].astype(BF16),
         out[tok_rows : tok_rows + top_count, :tok_rows].T,
-        *grads,
+        grad_gate.transpose(0, 2, 1),
+        grad_up.transpose(0, 2, 1),
+        grad_down,
     )
 
 

time: 156 us -> 109 us (0.70)
  the two profiles are of different devices: /device:TPU:26 before, /device:TPU:0 now
where the time goes in v3:
time: 109 us; the launch traced here: 108 us
  Pallas kernels  101 us (93%)
  other arithmetic  3.01 us (3%)
  local copies, waits for them, and re-layouts  2.96 us (3%)
    pallas_call x1, Pallas kernels, on_device(): pl.pallas_call(functools.partial(route_kernel, owners, run, slots, top_co...  83.7 us
    pallas_call x1, Pallas kernels, on_device(): pl.pallas_call(functools.partial(weights_kernel, hid, hid_pad), grid=(per...  17.7 us

profile of v3, /device:TPU:0, one launch (start us, length us, event | category | flops | bytes accessed | tf_op | source)
XLA Modules:
  0.0 108.0 jit_solution(10264175343673945588)
XLA Ops:
  0.6 0.7 convert_bitcast_fusion.1
  1.3 0.7 convert_bitcast_fusion
  2.0 1.6 %pad_maximum_fusion.tok_in = bf16[144,768]{1,0:T(8,128)(2,1)} fusion(bf16[16,768]{1,0:T(8,128)(2,1)S(1)} %fusion.2, bf16[128,768]{1,0:T(8,128)(2,1)} %param.7), kind=kLoop, calls=%fused_computation.1 | loop fusion | flops 442368 | bytes 442368 | tf_op jit(solution)/shard_map/concatenate | solution.py:473
  3.6 83.7 %route.1 = (f32[144,768]{1,0:T(8,128)}, bf16[16,160,768]{2,1,0:T(8,128)(2,1)}, bf16[16,160,768]{2,1,0:T(8,128)(2,1)}, bf16[16,160,768]{2,1,0:T(8,128)(2,1)}) custom-call(bf16[144,768]{1,0:T(8,128)(2,1)} %pad_maximum_fusion.tok_in, bf16[128,768]{1,0:T(8,128)(2,1)} %grad_in.1, bf16[16,192,768]{2,1,0:T(8,128)(2,1)} %bitcast.10, bf16[16,192,768]{2,1,0:T(8,128)(2,1)} %bitcast.11, ...), custom_call_target="tpu_custom_call" | custom-call | tf_op jit(solution)/shard_map/route/pallas_call | solution.py:477
  87.3 1.3 %slice_bitcast_fusion = f32[128,8]{0,1:T(8,128)} fusion(f32[144,768]{1,0:T(8,128)} %get-tuple-element.12), kind=kLoop, calls=%fused_computation.6 | loop fusion | bytes 8192 | tf_op jit(solution)/shard_map/transpose | solution.py:524
  88.6 1.7 %slice.12 = bf16[128,768]{1,0:T(8,128)(2,1)} slice(f32[144,768]{1,0:T(8,128)} %get-tuple-element.12), slice={[0:128], [0:768]} | slice | bytes 393216 | tf_op jit(solution)/shard_map/slice | solution.py:523
  90.3 17.7 %weight_grads.1 = (bf16[16,192,768]{2,1,0:T(8,128)(2,1)}, bf16[16,192,768]{2,1,0:T(8,128)(2,1)}, bf16[16,192,768]{2,1,0:T(8,128)(2,1)}) custom-call(bf16[16,160,768]{2,1,0:T(8,128)(2,1)} %get-tuple-element.13.xs, bf16[16,160,768]{2,1,0:T(8,128)(2,1)} %get-tuple-element.14.gs, bf16[16,160,768]{2,1,0:T(8,128)(2,1)} %get-tuple-element.15.back), custom_call_target="tpu_custom_call" | custom-call | tf_op jit(solution)/shard_map/weight_grads/pallas_call | solution.py:513
  (1 shorter events, 0.0 us)

commit v4 on v3

--- a/solution.py
+++ b/solution.py
@@ -416,10 +416,13 @@
 
 
 def weights_kernel(hid, hid_pad, xs, gs, back, gate_out, up_out, down_out):
-    rows_e = xs[0]
-    gate_out[0] = dot_t(back[0, :, 0:hid], rows_e, TRANS_LHS).astype(BF16)
-    up_out[0] = dot_t(back[0, :, hid_pad : hid_pad + hid], rows_e, TRANS_LHS).astype(BF16)
-    down_out[0] = dot_t(back[0, :, 2 * hid_pad : 2 * hid_pad + hid], gs[0], TRANS_LHS).astype(BF16)
+    for n in range(xs.shape[0]):
+        rows_e = xs[n]
+        gate_out[n] = dot_t(back[n, :, 0:hid], rows_e, TRANS_LHS).astype(BF16)
+        up_out[n] = dot_t(back[n, :, hid_pad : hid_pad + hid], rows_e, TRANS_LHS).astype(BF16)
+        down_out[n] = dot_t(
+            back[n, :, 2 * hid_pad : 2 * hid_pad + hid], gs[n], TRANS_LHS
+        ).astype(BF16)
 
 
 def on_device(tokens, out_grad, expert_ids, gate_probs, gate_weight, up_weight, down_weight):
@@ -507,12 +510,14 @@
         name="route",
     )(tok_in, out_grad, gate_weight.transpose(0, 2, 1), up_weight.transpose(0, 2, 1), down_weight)
 
+    batch = 4 if per_dev % 4 == 0 else 1
+
     def one(a, b):
-        return pl.BlockSpec((1, a, b), lambda e: (e, 0, 0))
+        return pl.BlockSpec((batch, a, b), lambda e: (e, 0, 0))
 
     grad_gate, grad_up, grad_down = pl.pallas_call(
         functools.partial(weights_kernel, hid, hid_pad),
-        grid=(per_dev,),
+        grid=(per_dev // batch,),
         out_shape=(jax.ShapeDtypeStruct(down_weight.shape, BF16),) * 3,
         in_specs=[one(rows, width), one(rows, width), one(rows, 3 * hid_pad)],
         out_specs=(one(hid, width),) * 3,

time: 109 us -> 101 us (0.927); the launches traced: 108 us -> 101 us
  Pallas kernels: 101 us -> 94.5 us
    pallas_call x1, Pallas kernels: 17.7 us -> 10.8 us  [on_device(): pl.pallas_call(functools.partial(weights_kernel, hid, hid_pad), grid=(per...]
where the time goes in v4:
time: 101 us
  Pallas kernels  94.5 us (94%)
  other arithmetic  3.01 us (3%)
  local copies, waits for them, and re-layouts  2.96 us (3%)
    pallas_call x1, Pallas kernels, on_device(): pl.pallas_call(functools.partial(route_kernel, owners, run, slots, top_co...  83.7 us
    pallas_call x1, Pallas kernels, on_device(): pl.pallas_call(functools.partial(weights_kernel, hid, hid_pad), grid=(per...  10.8 us

profile of v4, /device:TPU:0, one launch (start us, length us, event | category | flops | bytes accessed | tf_op | source)
XLA Modules:
  0.0 101.1 jit_solution(13183216701982402343)
XLA Ops:
  0.6 0.7 convert_bitcast_fusion.1
  1.3 0.7 convert_bitcast_fusion
  2.0 1.6 %pad_maximum_fusion.tok_in = bf16[144,768]{1,0:T(8,128)(2,1)} fusion(bf16[16,768]{1,0:T(8,128)(2,1)S(1)} %fusion.2, bf16[128,768]{1,0:T(8,128)(2,1)} %param.7), kind=kLoop, calls=%fused_computation.1 | loop fusion | flops 442368 | bytes 442368 | tf_op jit(solution)/shard_map/concatenate | solution.py:476
  3.6 83.7 %route.1 = (f32[144,768]{1,0:T(8,128)}, bf16[16,160,768]{2,1,0:T(8,128)(2,1)}, bf16[16,160,768]{2,1,0:T(8,128)(2,1)}, bf16[16,160,768]{2,1,0:T(8,128)(2,1)}) custom-call(bf16[144,768]{1,0:T(8,128)(2,1)} %pad_maximum_fusion.tok_in, bf16[128,768]{1,0:T(8,128)(2,1)} %grad_in.1, bf16[16,192,768]{2,1,0:T(8,128)(2,1)} %bitcast.10, bf16[16,192,768]{2,1,0:T(8,128)(2,1)} %bitcast.11, ...), custom_call_target="tpu_custom_call" | custom-call | tf_op jit(solution)/shard_map/route/pallas_call | solution.py:480
  87.3 1.3 %slice_bitcast_fusion = f32[128,8]{0,1:T(8,128)} fusion(f32[144,768]{1,0:T(8,128)} %get-tuple-element.12), kind=kLoop, calls=%fused_computation.6 | loop fusion | bytes 8192 | tf_op jit(solution)/shard_map/transpose | solution.py:529
  88.6 1.7 %slice.12 = bf16[128,768]{1,0:T(8,128)(2,1)} slice(f32[144,768]{1,0:T(8,128)} %get-tuple-element.12), slice={[0:128], [0:768]} | slice | bytes 393216 | tf_op jit(solution)/shard_map/slice | solution.py:528
  90.3 10.8 %weight_grads.1 = (bf16[16,192,768]{2,1,0:T(8,128)(2,1)}, bf16[16,192,768]{2,1,0:T(8,128)(2,1)}, bf16[16,192,768]{2,1,0:T(8,128)(2,1)}) custom-call(bf16[16,160,768]{2,1,0:T(8,128)(2,1)} %get-tuple-element.13.xs, bf16[16,160,768]{2,1,0:T(8,128)(2,1)} %get-tuple-element.14.gs, bf16[16,160,768]{2,1,0:T(8,128)(2,1)} %get-tuple-element.15.back), custom_call_target="tpu_custom_call" | custom-call | tf_op jit(solution)/shard_map/weight_grads/pallas_call | solution.py:518
  (1 shorter events, 0.0 us)
